TPU v7x, 128 devices: a whole 4x4x4 slice. The times are simulated.
128 devices in a mesh: leaf: 8 (over x, core), prow: 4 (over z), pcol: 4 (over y).
Axes of the slice: x: 4, y: 4, z: 4, core: 2. Of those that a mesh axis runs over, the one named last changes fastest.
Arguments:
- subtree_factor: float32 [8, 2, 8, 256, 2048], P('leaf', None, None, 'prow', 'pcol'), may hold values from -0.09375 to 0.09375
- sub_linv: float32 [8, 2, 8, 256, 256], P('leaf', None, None, 'prow'), may hold values from -0.05 to 1.05
- sub_uinv: float32 [8, 2, 8, 256, 256], P('leaf', None, None, 'prow'), may hold values from -0.05 to 1.05
- lower_panel: float32 [8, 4, 256, 2, 2048], P('leaf', None, 'prow', None, 'pcol'), may hold values from -0.0234375 to 0.0234375
- upper_panel: float32 [8, 2, 8, 256, 1024], P('leaf', None, None, 'prow', 'pcol'), may hold values from -0.125 to 0.125
- panel_rows: int32 [8, 4, 2], P('leaf'), may hold values 0 or 1
- upper_level_factor: float32 [4, 256, 1024], P(None, 'prow', 'pcol'), may hold values from -0.125 to 0.125
- top_linv: float32 [4, 256, 256], P(None, 'prow'), may hold values from -0.05 to 1.05
- top_uinv: float32 [4, 256, 256], P(None, 'prow'), may hold values from -0.05 to 1.05
- sub_rhs: float32 [8, 2, 8, 256, 256], P('leaf', None, None, 'prow'), may hold values from -6 to 6
- top_rhs: float32 [4, 256, 256], P(None, 'prow', 'leaf'), may hold values from -6 to 6
Outputs:
- sub_solution: float32 [8, 2, 8, 256, 256], P('leaf', None, 'pcol')
- top_solution: float32 [4, 256, 256], P('pcol', None, 'leaf')
All inputs are finite; a program needn't handle non-finite values. No bound on the sum of `panel_rows` on one device may be relied on, other than what follows from the above.
Results may differ from a plain program's by a relative error of at most 0.00013.
Values sent between devices are 32-bit elements; how exact they have to be, the bound alone decides.
A program may use at most 128 MiB of HBM per device.

v0:
```python
import jax
import jax.numpy as jnp
from jax import lax
from jax.sharding import PartitionSpec as P

TOP_PRECISION = lax.Precision.HIGHEST


def block_order(block_count, forward):
    return range(block_count) if forward else range(block_count - 1, -1, -1)


def sweep_blocks(factor_row_block, inverses, right_side, coupling, owned_start, my_col, forward):
    groups, block_count, tile_rows, columns = right_side.shape
    block_rows = inverses.shape[3]
    owned_count = factor_row_block.shape[3] // block_rows
    solved = jnp.zeros((groups, block_count, block_rows, columns), jnp.float32)
    for sweep_step_index in block_order(block_count, forward):
        held_value_entries = lax.dynamic_slice_in_dim(solved, owned_start, owned_count, 1)
        held_value_entries = held_value_entries.reshape(groups, owned_count * block_rows, columns)
        partial_value = coupling[:, sweep_step_index] + jnp.einsum(
            "pht,ptj->phj",
            factor_row_block[:, sweep_step_index],
            held_value_entries,
            precision=TOP_PRECISION,
        )
        local_side = jnp.where(my_col == 0, right_side[:, sweep_step_index], 0.0) - partial_value
        inverse_part = jnp.einsum(
            "gab,gar->gbr", inverses[:, sweep_step_index], local_side, precision=TOP_PRECISION
        )
        block_value = lax.psum(inverse_part, ("prow", "pcol"))
        solved = solved.at[:, sweep_step_index].set(block_value)
    return solved


def per_device(
    subtree_factor,
    sub_linv,
    sub_uinv,
    lower_panel,
    upper_panel,
    panel_rows,
    upper_level_factor,
    top_linv,
    top_uinv,
    sub_rhs,
    top_rhs,
):
    my_row = lax.axis_index("prow")
    my_col = lax.axis_index("pcol")
    block_rows = sub_linv.shape[4]
    tile_rows = sub_rhs.shape[3]
    groups = sub_rhs.shape[1]
    block_count = sub_rhs.shape[2]
    sub_owned = subtree_factor.shape[4] // block_rows
    top_owned = upper_level_factor.shape[2] // block_rows
    present = panel_rows[0].astype(jnp.float32)
    linv_rows, uinv_rows, top_linv_rows, top_uinv_rows = (sub_linv, sub_uinv, top_linv, top_uinv)
    lower_sub = sweep_blocks(
        subtree_factor[0],
        linv_rows[0],
        sub_rhs[0],
        jnp.zeros(sub_rhs[0].shape, jnp.float32),
        my_col * sub_owned,
        my_col,
        True,
    )
    lower_owned = lax.dynamic_slice_in_dim(lower_sub, my_col * sub_owned, sub_owned, 1)
    lower_owned = lower_owned.reshape(groups, sub_owned * block_rows, lower_sub.shape[3])
    contrib_part = jnp.einsum(
        "tasm,ts,smr->tar", lower_panel[0], present, lower_owned, precision=TOP_PRECISION
    )
    contrib = lax.psum(contrib_part, "leaf")
    upper_level_side = lax.all_gather(top_rhs, "leaf", axis=2, tiled=True)
    upper_level_lower = sweep_blocks(
        upper_level_factor[None],
        top_linv_rows[None],
        upper_level_side[None],
        contrib[None],
        my_col * top_owned,
        my_col,
        True,
    )
    top_rows = lax.dynamic_slice_in_dim(upper_level_lower, my_row * tile_rows, tile_rows, 2)
    top_upper = sweep_blocks(
        upper_level_factor[None],
        top_uinv_rows[None],
        top_rows,
        jnp.zeros(top_rows.shape, jnp.float32),
        my_col * top_owned,
        my_col,
        False,
    )[0]
    top_out = lax.dynamic_slice_in_dim(
        top_upper, lax.axis_index("leaf") * top_rhs.shape[2], top_rhs.shape[2], 2
    )
    top_out = lax.dynamic_slice_in_dim(top_out, my_col * top_owned, top_owned, 0)
    top_mine = lax.dynamic_slice_in_dim(top_upper, my_col * top_owned, top_owned, 0)
    mask_mine = lax.dynamic_slice_in_dim(present, my_col * top_owned, top_owned, 0)
    upper_local = upper_panel[0].reshape(groups, block_count, tile_rows, top_owned, block_rows)
    coupling = jnp.einsum(
        "skatb,ts,tbr->skar", upper_local, mask_mine, top_mine, precision=TOP_PRECISION
    )
    sub_rows = lax.dynamic_slice_in_dim(lower_sub, my_row * tile_rows, tile_rows, 2)
    upper_sub = sweep_blocks(
        subtree_factor[0], uinv_rows[0], sub_rows, coupling, my_col * sub_owned, my_col, False
    )
    sub_out = lax.dynamic_slice_in_dim(upper_sub, my_col * sub_owned, sub_owned, 1)
    return (sub_out[None], top_out)


def solution(mesh):
    placed = (
        P("leaf", None, None, "prow", "pcol"),
        P("leaf", None, None, "prow", None),
        P("leaf", None, None, "prow", None),
        P("leaf", None, "prow", None, "pcol"),
        P("leaf", None, None, "prow", "pcol"),
        P("leaf", None, None),
        P(None, "prow", "pcol"),
        P(None, "prow", None),
        P(None, "prow", None),
        P("leaf", None, None, "prow", None),
        P(None, "prow", "leaf"),
    )
    return jax.shard_map(
        per_device,
        mesh=mesh,
        in_specs=placed,
        out_specs=(P("leaf", None, "pcol", None, None), P("pcol", None, "leaf")),
        check_vma=False,
    )
```

profile of v0, /device:TPU:0, one launch (start us, length us, event | category | flops | bytes accessed | tf_op | source)
XLA Modules:
  0.0 2303.5 jit_solution(17855429060302195027)
XLA Ops:
  15.9 88.4 %all-reduce.30.cloned.1.call-done = f32[2,1,256,256]{3,2,0,1:T(8,128)} async-done(((f32[2,1,256,256]{3,2,0,1:T(8,128)}), f32[2,1,256,256]{3,2,0,1:T(8,128)}) %all-reduce.30.cloned.1.call-update) | async-done | bytes 524304 | tf_op jit(solution)/shard_map/psum | solution.py:31
  109.6 3.4 scatter.80
  113.0 80.7 %all-reduce.32.cloned.1.call-done = f32[2,1,256,256]{3,2,0,1:T(8,128)} async-done(((f32[2,1,256,256]{3,2,0,1:T(8,128)}), f32[2,1,256,256]{3,2,0,1:T(8,128)}) %all-reduce.32.cloned.1.call-update) | async-done | bytes 524304 | tf_op jit(solution)/shard_map/psum | solution.py:31
  201.2 85.3 %all-reduce.34.cloned.1.call-done = f32[2,1,256,256]{3,2,0,1:T(8,128)} async-done(((f32[2,1,256,256]{3,2,0,1:T(8,128)}), f32[2,1,256,256]{3,2,0,1:T(8,128)}) %all-reduce.34.cloned.1.call-update) | async-done | bytes 524304 | tf_op jit(solution)/shard_map/psum | solution.py:31
  293.9 85.3 %all-reduce.36.cloned.1.call-done = f32[2,1,256,256]{3,2,0,1:T(8,128)} async-done(((f32[2,1,256,256]{3,2,0,1:T(8,128)}), f32[2,1,256,256]{3,2,0,1:T(8,128)}) %all-reduce.36.cloned.1.call-update) | async-done | bytes 524304 | tf_op jit(solution)/shard_map/psum | solution.py:31
  386.6 85.3 %all-reduce.38.cloned.1.call-done = f32[2,1,256,256]{3,2,0,1:T(8,128)} async-done(((f32[2,1,256,256]{3,2,0,1:T(8,128)}), f32[2,1,256,256]{3,2,0,1:T(8,128)}) %all-reduce.38.cloned.1.call-update) | async-done | bytes 524304 | tf_op jit(solution)/shard_map/psum | solution.py:31
  479.3 85.2 %all-reduce.40.cloned.1.call-done = f32[2,1,256,256]{3,2,0,1:T(8,128)} async-done(((f32[2,1,256,256]{3,2,0,1:T(8,128)}), f32[2,1,256,256]{3,2,0,1:T(8,128)}) %all-reduce.40.cloned.1.call-update) | async-done | bytes 524304 | tf_op jit(solution)/shard_map/psum | solution.py:31
  572.0 85.3 %all-reduce.42.cloned.1.call-done = f32[2,1,256,256]{3,2,0,1:T(8,128)} async-done(((f32[2,1,256,256]{3,2,0,1:T(8,128)}), f32[2,1,256,256]{3,2,0,1:T(8,128)}) %all-reduce.42.cloned.1.call-update) | async-done | bytes 524304 | tf_op jit(solution)/shard_map/psum | solution.py:31
  665.0 2.6 fusion.33
  667.6 82.2 %all-reduce.44.cloned.1.call-done = f32[2,1,256,256]{3,2,0,1:T(8,128)} async-done(((f32[2,1,256,256]{3,2,0,1:T(8,128)}), f32[2,1,256,256]{3,2,0,1:T(8,128)}) %all-reduce.44.cloned.1.call-update) | async-done | bytes 524304 | tf_op jit(solution)/shard_map/psum | solution.py:31
  755.1 14.6 all_gather.3
  771.9 42.9 %all-reduce.46.cloned.1.call-done = f32[1,4,64,256]{3,2,1,0:T(8,128)} async-done(((f32[1,4,64,256]{3,2,1,0:T(8,128)}), f32[1,4,64,256]{3,2,1,0:T(8,128)}) %all-reduce.46.cloned.1.call-update) | async-done | bytes 262160 | tf_op jit(solution)/shard_map/psum | solution.py:73
  816.8 85.7 %all-reduce.48.cloned.1.call-done = f32[1,1,256,256]{3,2,1,0:T(8,128)} async-done(((f32[1,1,256,256]{3,2,1,0:T(8,128)}), f32[1,1,256,256]{3,2,1,0:T(8,128)}) %all-reduce.48.cloned.1.call-update) | async-done | bytes 262160 | tf_op jit(solution)/shard_map/psum | solution.py:31
  907.9 82.4 %all-reduce.50.cloned.1.call-done = f32[1,1,256,256]{3,2,1,0:T(8,128)} async-done(((f32[1,1,256,256]{3,2,1,0:T(8,128)}), f32[1,1,256,256]{3,2,1,0:T(8,128)}) %all-reduce.50.cloned.1.call-update) | async-done | bytes 262160 | tf_op jit(solution)/shard_map/psum | solution.py:31
  995.2 84.5 %all-reduce.52.cloned.1.call-done = f32[1,1,256,256]{3,2,1,0:T(8,128)} async-done(((f32[1,1,256,256]{3,2,1,0:T(8,128)}), f32[1,1,256,256]{3,2,1,0:T(8,128)}) %all-reduce.52.cloned.1.call-update) | async-done | bytes 262160 | tf_op jit(solution)/shard_map/psum | solution.py:31
  1084.7 84.5 %all-reduce.54.cloned.1.call-done = f32[1,1,256,256]{3,2,1,0:T(8,128)} async-done(((f32[1,1,256,256]{3,2,1,0:T(8,128)}), f32[1,1,256,256]{3,2,1,0:T(8,128)}) %all-reduce.54.cloned.1.call-update) | async-done | bytes 262160 | tf_op jit(solution)/shard_map/psum | solution.py:31
  1173.0 84.5 %all-reduce.56.cloned.1.call-done = f32[1,1,256,256]{2,3,1,0:T(8,128)} async-done(((f32[1,1,256,256]{2,3,1,0:T(8,128)}), f32[1,1,256,256]{2,3,1,0:T(8,128)}) %all-reduce.56.cloned.1.call-update) | async-done | bytes 262160 | tf_op jit(solution)/shard_map/psum | solution.py:31
  1262.8 82.5 %all-reduce.58.cloned.1.call-done = f32[1,1,256,256]{2,3,1,0:T(8,128)} async-done(((f32[1,1,256,256]{2,3,1,0:T(8,128)}), f32[1,1,256,256]{2,3,1,0:T(8,128)}) %all-reduce.58.cloned.1.call-update) | async-done | bytes 262160 | tf_op jit(solution)/shard_map/psum | solution.py:31
  1350.3 84.5 %all-reduce.60.cloned.1.call-done = f32[1,1,256,256]{2,3,1,0:T(8,128)} async-done(((f32[1,1,256,256]{2,3,1,0:T(8,128)}), f32[1,1,256,256]{2,3,1,0:T(8,128)}) %all-reduce.60.cloned.1.call-update) | async-done | bytes 262160 | tf_op jit(solution)/shard_map/psum | solution.py:31
  1442.3 82.0 %all-reduce.62.cloned.1.call-done = f32[1,256,256]{1,2,0:T(8,128)} async-done(((f32[1,256,256]{1,2,0:T(8,128)}), f32[1,256,256]{1,2,0:T(8,128)}) %all-reduce.62.cloned.1.call-update) | async-done | bytes 262160 | tf_op jit(solution)/shard_map/psum | solution.py:31
  1534.6 85.1 %all-reduce.64.cloned.1.call-done = f32[2,1,256,256]{2,3,0,1:T(8,128)} async-done(((f32[2,1,256,256]{2,3,0,1:T(8,128)}), f32[2,1,256,256]{2,3,0,1:T(8,128)}) %all-reduce.64.cloned.1.call-update) | async-done | bytes 524304 | tf_op jit(solution)/shard_map/psum | solution.py:31
  1621.9 2.6 copy.114
  1629.1 3.4 scatter.106
  1632.5 81.6 %all-reduce.66.cloned.1.call-done = f32[2,1,256,256]{2,3,0,1:T(8,128)} async-done(((f32[2,1,256,256]{2,3,0,1:T(8,128)}), f32[2,1,256,256]{2,3,0,1:T(8,128)}) %all-reduce.66.cloned.1.call-update) | async-done | bytes 524304 | tf_op jit(solution)/shard_map/psum | solution.py:31
  1718.2 2.5 copy.115
  1725.3 85.2 %all-reduce.68.cloned.1.call-done = f32[2,1,256,256]{2,3,0,1:T(8,128)} async-done(((f32[2,1,256,256]{2,3,0,1:T(8,128)}), f32[2,1,256,256]{2,3,0,1:T(8,128)}) %all-reduce.68.cloned.1.call-update) | async-done | bytes 524304 | tf_op jit(solution)/shard_map/psum | solution.py:31
  1814.6 2.5 copy.116
  1821.7 85.2 %all-reduce.70.cloned.1.call-done = f32[2,1,256,256]{2,3,0,1:T(8,128)} async-done(((f32[2,1,256,256]{2,3,0,1:T(8,128)}), f32[2,1,256,256]{2,3,0,1:T(8,128)}) %all-reduce.70.cloned.1.call-update) | async-done | bytes 524304 | tf_op jit(solution)/shard_map/psum | solution.py:31
  1918.0 85.2 %all-reduce.72.cloned.1.call-done = f32[2,1,256,256]{2,3,0,1:T(8,128)} async-done(((f32[2,1,256,256]{2,3,0,1:T(8,128)}), f32[2,1,256,256]{2,3,0,1:T(8,128)}) %all-reduce.72.cloned.1.call-update) | async-done | bytes 524304 | tf_op jit(solution)/shard_map/psum | solution.py:31
  2014.4 85.3 %all-reduce.74.cloned.1.call-done = f32[2,1,256,256]{2,3,0,1:T(8,128)} async-done(((f32[2,1,256,256]{2,3,0,1:T(8,128)}), f32[2,1,256,256]{2,3,0,1:T(8,128)}) %all-reduce.74.cloned.1.call-update) | async-done | bytes 524304 | tf_op jit(solution)/shard_map/psum | solution.py:31
  2110.9 85.2 %all-reduce.76.cloned.1.call-done = f32[2,1,256,256]{2,3,0,1:T(8,128)} async-done(((f32[2,1,256,256]{2,3,0,1:T(8,128)}), f32[2,1,256,256]{2,3,0,1:T(8,128)}) %all-reduce.76.cloned.1.call-update) | async-done | bytes 524304 | tf_op jit(solution)/shard_map/psum | solution.py:31
  2208.7 83.8 %all-reduce.78.cloned.1.call-done = f32[2,1,256,256]{2,3,0,1:T(8,128)} async-done(((f32[2,1,256,256]{2,3,0,1:T(8,128)}), f32[2,1,256,256]{2,3,0,1:T(8,128)}) %all-reduce.78.cloned.1.call-update) | async-done | bytes 524304 | tf_op jit(solution)/shard_map/psum | solution.py:31
  (176 shorter events, 189.8 us)
Async XLA Ops:
  7.2 1521.5 %copy-start = (f32[1,2,8,64,256]{4,3,2,1,0:T(8,128)S(1)}, f32[1,2,8,64,256]{4,3,2,1,0:T(8,128)}, u32[]{:S(2)}) copy-start(f32[1,2,8,64,256]{4,3,2,1,0:T(8,128)} %param.63) | copy-start | bytes 3145732
  7.2 97.1 %all-reduce.30.cloned.1.call-start = ((), (), s32[]{:S(2)}) async-start(), calls=%async_computation | async-start | bytes 1048576 | tf_op jit(solution)/shard_map/psum | solution.py:31
  7.2 4.7 copy-start.3
  15.8 177.9 %all-reduce.32.cloned.1.call-start = ((), (), s32[]{:S(2)}) async-start(), calls=%async_computation.1 | async-start | bytes 1048576 | tf_op jit(solution)/shard_map/psum | solution.py:31
  109.6 176.9 %all-reduce.34.cloned.1.call-start = ((), (), s32[]{:S(2)}) async-start(), calls=%async_computation.2 | async-start | bytes 1048576 | tf_op jit(solution)/shard_map/psum | solution.py:31
  201.1 178.0 %all-reduce.36.cloned.1.call-start = ((), (), s32[]{:S(2)}) async-start(), calls=%async_computation.3 | async-start | bytes 1048576 | tf_op jit(solution)/shard_map/psum | solution.py:31
  293.9 178.0 %all-reduce.38.cloned.1.call-start = ((), (), s32[]{:S(2)}) async-start(), calls=%async_computation.4 | async-start | bytes 1048576 | tf_op jit(solution)/shard_map/psum | solution.py:31
  386.6 177.9 %all-reduce.40.cloned.1.call-start = ((), (), s32[]{:S(2)}) async-start(), calls=%async_computation.5 | async-start | bytes 1048576 | tf_op jit(solution)/shard_map/psum | solution.py:31
  479.3 177.9 %all-reduce.42.cloned.1.call-start = ((), (), s32[]{:S(2)}) async-start(), calls=%async_computation.6 | async-start | bytes 1048576 | tf_op jit(solution)/shard_map/psum | solution.py:31
  571.9 92.9 %copy-start.6 = (s32[1,4,2]{1,2,0:T(2,128)S(1)}, s32[1,4,2]{1,2,0:T(2,128)}, u32[]{:S(2)}) copy-start(s32[1,4,2]{1,2,0:T(2,128)} %param.64) | copy-start | bytes 100
  571.9 93.0 %copy-start.5 = (f32[4,64,32]{1,2,0:T(8,128)S(1)}, f32[4,64,32]{1,2,0:T(8,128)}, u32[]{:S(2)}) copy-start(f32[4,64,32]{1,2,0:T(8,128)} %param.69) | copy-start | bytes 98308
  571.9 177.9 %all-reduce.44.cloned.1.call-start = ((), (), s32[]{:S(2)}) async-start(), calls=%async_computation.7 | async-start | bytes 1048576 | tf_op jit(solution)/shard_map/psum | solution.py:31
  664.6 150.2 %all-reduce.46.cloned.1.call-start = ((), (), s32[]{:S(2)}) async-start(), calls=%async_computation.8 | async-start | bytes 524288 | tf_op jit(solution)/shard_map/psum | solution.py:73
  749.8 3.4 copy-start.1
  755.0 147.5 %all-reduce.48.cloned.1.call-start = ((), (), s32[]{:S(2)}) async-start(), calls=%async_computation.9 | async-start | bytes 524288 | tf_op jit(solution)/shard_map/psum | solution.py:31
  816.8 173.4 %all-reduce.50.cloned.1.call-start = ((), (), s32[]{:S(2)}) async-start(), calls=%async_computation.10 | async-start | bytes 524288 | tf_op jit(solution)/shard_map/psum | solution.py:31
  905.8 173.9 %all-reduce.52.cloned.1.call-start = ((), (), s32[]{:S(2)}) async-start(), calls=%async_computation.11 | async-start | bytes 524288 | tf_op jit(solution)/shard_map/psum | solution.py:31
  995.1 174.0 %all-reduce.54.cloned.1.call-start = ((), (), s32[]{:S(2)}) async-start(), calls=%async_computation.12 | async-start | bytes 524288 | tf_op jit(solution)/shard_map/psum | solution.py:31
  1082.6 264.3 %copy-start.4 = (f32[4,64,256]{2,1,0:T(8,128)S(1)}, f32[4,64,256]{2,1,0:T(8,128)}, u32[]{:S(2)}) copy-start(f32[4,64,256]{2,1,0:T(8,128)} %param.65) | copy-start | bytes 786436
  1084.7 172.8 %all-reduce.56.cloned.1.call-start = ((), (), s32[]{:S(2)}) async-start(), calls=%async_computation.13 | async-start | bytes 524288 | tf_op jit(solution)/shard_map/psum | solution.py:31
  1172.9 172.3 %all-reduce.58.cloned.1.call-start = ((), (), s32[]{:S(2)}) async-start(), calls=%async_computation.14 | async-start | bytes 524288 | tf_op jit(solution)/shard_map/psum | solution.py:31
  1260.7 174.1 %all-reduce.60.cloned.1.call-start = ((), (), s32[]{:S(2)}) async-start(), calls=%async_computation.15 | async-start | bytes 524288 | tf_op jit(solution)/shard_map/psum | solution.py:31
  1350.2 174.0 %all-reduce.62.cloned.1.call-start = ((), (), s32[]{:S(2)}) async-start(), calls=%async_computation.16 | async-start | bytes 524288 | tf_op jit(solution)/shard_map/psum | solution.py:31
  1439.8 180.0 %all-reduce.64.cloned.1.call-start = ((), (), s32[]{:S(2)}) async-start(), calls=%async_computation.17 | async-start | bytes 1048576 | tf_op jit(solution)/shard_map/psum | solution.py:31
  1529.9 1.1 copy-start.2
  1534.6 179.5 %all-reduce.66.cloned.1.call-start = ((), (), s32[]{:S(2)}) async-start(), calls=%async_computation.18 | async-start | bytes 1048576 | tf_op jit(solution)/shard_map/psum | solution.py:31
  1628.9 181.6 %all-reduce.68.cloned.1.call-start = ((), (), s32[]{:S(2)}) async-start(), calls=%async_computation.19 | async-start | bytes 1048576 | tf_op jit(solution)/shard_map/psum | solution.py:31
  1725.2 181.6 %all-reduce.70.cloned.1.call-start = ((), (), s32[]{:S(2)}) async-start(), calls=%async_computation.20 | async-start | bytes 1048576 | tf_op jit(solution)/shard_map/psum | solution.py:31
  1821.6 181.6 %all-reduce.72.cloned.1.call-start = ((), (), s32[]{:S(2)}) async-start(), calls=%async_computation.21 | async-start | bytes 1048576 | tf_op jit(solution)/shard_map/psum | solution.py:31
  1918.0 181.7 %all-reduce.74.cloned.1.call-start = ((), (), s32[]{:S(2)}) async-start(), calls=%async_computation.22 | async-start | bytes 1048576 | tf_op jit(solution)/shard_map/psum | solution.py:31
  2014.3 181.7 %all-reduce.76.cloned.1.call-start = ((), (), s32[]{:S(2)}) async-start(), calls=%async_computation.23 | async-start | bytes 1048576 | tf_op jit(solution)/shard_map/psum | solution.py:31
  2110.8 181.7 %all-reduce.78.cloned.1.call-start = ((), (), s32[]{:S(2)}) async-start(), calls=%async_computation.24 | async-start | bytes 1048576 | tf_op jit(solution)/shard_map/psum | solution.py:31
Sparse Core Ops, SparseCore 0:
  15.9 88.3 all-reduce.29
  109.7 84.0 all-reduce.31
  201.3 85.1 all-reduce.33
  294.0 85.1 all-reduce.35
  386.7 85.1 all-reduce.37
  479.4 85.0 all-reduce.39
  572.0 85.1 all-reduce.41
  664.7 85.0 all-reduce.43
  755.1 59.5 all-reduce.45
  818.3 84.1 all-reduce.47
  905.9 84.2 all-reduce.49
  995.3 84.3 all-reduce.51
  1084.8 84.3 all-reduce.53
  1173.1 84.3 all-reduce.55
  1260.8 84.3 all-reduce.57
  1350.4 84.3 all-reduce.59
  1439.9 84.3 all-reduce.61
  1534.7 85.0 all-reduce.63
  1629.0 85.0 all-reduce.65
  1725.3 85.0 all-reduce.67
  1821.7 85.0 all-reduce.69
  1918.1 85.0 all-reduce.71
  2014.5 85.1 all-reduce.73
  2110.9 85.0 all-reduce.75
  2207.4 85.0 all-reduce.77
where the time goes:
time: 2310 us; the launch traced here: 2300 us
  waiting for transfers between devices  2070 us (90%)
  local copies, waits for them, and re-layouts  108 us (5%)
  matrix products  93 us (4%)
    psum x24, waiting for transfers between devices, sweep_blocks(): block_value = lax.psum(inverse_part, ('prow', 'pcol'))  2020 us
    dot_general x24, matrix products, sweep_blocks(): jnp.einsum('gab,gar->gbr', inverses[:, sweep_step_index], local_side, pre...  53.3 us
    scatter x24, local copies, waits for them, and re-layouts, sweep_blocks(): solved = solved.at[:, sweep_step_index].set(block_value)  47.2 us
  transfers between devices with their start and end apart: 25, of which 25 were waited for; matrix products, arithmetic and copies ran while one was open for 1% of the time, Pallas kernels for 0%

commit v1 on v0

v1 whole, which is shorter than its diff:
```python
import jax
import jax.numpy as jnp
from jax import lax
from jax.experimental import pallas as pl
from jax.experimental.pallas import tpu as pltpu
from jax.sharding import PartitionSpec as P

MESH = pl.DeviceIdType.MESH
F32 = jnp.float32
BF16 = jnp.bfloat16
NPOS = 18
SEND_AT = {-1: (0, 1, 2), 0: (3,), 1: (4,), 2: (5,), 3: (6, 7), 4: (8,), 5: (9,), 6: (10,), 7: (11, 12), 8: (13,), 9: (14,), 10: (15,), 11: (16,), 12: (17,)}
RELAY_AT = {0: (0, 1), 1: (2,), 2: (3,), 3: (4,), 4: (5,), 5: (6, 7), 6: (8,), 7: (9, 10), 8: (11, 12), 9: (13,), 10: (14,), 11: (15,), 12: (16,), 13: (17,)}
ARRIVE_AT = {0: (0,), 1: (1,), 2: (2,), 3: (3,), 4: (4,), 5: (5,), 6: (6,), 7: (7, 8), 8: (11, 12), 10: (13,), 11: (14,), 12: (15,), 13: (16,), 14: (17,)}


def halves(value):
    high = value.astype(BF16)
    return high, (value - high.astype(F32)).astype(BF16)


def product(left, right):
    def one(a, b):
        return jnp.dot(a, b, preferred_element_type=F32)

    return one(left[0], right[0]) + (one(left[0], right[1]) + one(left[1], right[0]))


def kernel(
    present_ref,
    factor,
    linv,
    uinv,
    lower,
    upper,
    topf,
    tlinv,
    tuinv,
    rhs,
    toprhs,
    sub_out,
    top_out,
    slab,
    lowers,
    uppers,
    tops,
    inv,
    base,
    gath,
    sol,
    solh,
    soll,
    invh,
    invl,
    coup,
    part,
    red,
    trhs,
    swap,
    ssem_y,
    rsem_y,
    ssem_i,
    rsem_i,
    ssem_g,
    rsem_g,
    ssem_r,
    rsem_r,
    ssem_a,
    rsem_a,
    ssem_o,
    rsem_o,
    misc,
    ssem_x,
    rsem_x,
):
    leaf = lax.axis_index("leaf")
    row = lax.axis_index("prow")
    col = lax.axis_index("pcol")
    sub = col // 2
    half = lax.rem(col + sub, 2)
    beside = col + 1 - 2 * lax.rem(col, 2)
    across = 3 - col
    rows = pl.ds(pl.multiple_of(row * 64, 64), 64)

    def zpeer(d):
        return (leaf, lax.rem(row + d, 4), col)

    def ypeer(c):
        return (leaf, row, c)

    group = []
    for other in (0, 1):
        for d in range(8):
            if other or d:
                group.append((other, d))

    def member(other, d):
        there = lax.rem(leaf + d, 8)
        return (there, row, across if other else col), (1 - sub if other else sub) * 8 + there

    barrier = pltpu.get_barrier_semaphore()
    greeted = [zpeer(d) for d in (1, 2, 3)]
    greeted += [ypeer(beside), ypeer(3 - beside)]
    greeted += [member(o, d)[0] for o, d in group]
    for peer in greeted:
        pl.semaphore_signal(barrier, inc=1, device_id=peer, device_id_type=MESH)
    pl.semaphore_wait(barrier, len(greeted))

    def remote(src, dst, send, recv, peer):
        return pltpu.make_async_remote_copy(
            src_ref=src, dst_ref=dst, send_sem=send, recv_sem=recv, device_id=peer, device_id_type=MESH
        )

    def arrived(ref, sem):
        pltpu.make_async_copy(ref, ref, sem).wait()

    def piece(owner, p):
        near = 7 - 2 * owner
        if p < near:
            i = 2 * owner + 1 + p
            if p == 0:
                return lambda s: factor.at[s, i, :, pl.ds(0, 256)], slab.at[owner, i, :, pl.ds(0, 256)]
            return lambda s: factor.at[s, i], slab.at[owner, i]
        if p < near + 4:
            t = p - near
            return lambda s: lower.at[s, t], lowers.at[owner, t]
        if p < near + 6:
            t = pl.ds(2 * (p - near - 4), 2)
            return lambda s: topf.at[t], tops.at[owner, t]
        if p < near + 10:
            i = pl.ds(2 * (p - near - 6), 2)
            return lambda s: upper.at[s, i], uppers.at[owner, i]
        i = 2 * owner - (p - near - 10)
        return lambda s: factor.at[s, i], slab.at[owner, i]

    def travel(sends=(), relays=(), arrivals=(), first=False, last=False):
        for o in range(4):
            mine, there, over = o // 2, 1 - o // 2, 3 - o

            @pl.when(col == o)
            def _():
                if first:
                    for p in range(NPOS):
                        src, dst = piece(o, p)
                        pltpu.make_async_copy(src(mine), dst, rsem_y.at[p, o]).start()
                for p in sends:
                    src, dst = piece(o, p)
                    remote(src(mine), dst, ssem_y.at[p, 0], rsem_y.at[p, o], ypeer(o ^ 1)).start()
                    remote(src(there), dst, ssem_y.at[p, 1], rsem_y.at[p, o], ypeer(over)).start()
                for p in relays:
                    dst = piece(over, p)[1]
                    arrived(dst, rsem_y.at[p, over])
                    remote(dst, dst, ssem_y.at[p, 2], rsem_y.at[p, over], ypeer(o ^ 1)).start()
                for p in arrivals:
                    for other in (o, o ^ 1, 3 - (o ^ 1)):
                        arrived(piece(other, p)[1], rsem_y.at[p, other])
                if last:
                    for p in range(NPOS):
                        dst = piece(o, p)[1]
                        arrived(dst, ssem_y.at[p, 0])
                        arrived(dst, ssem_y.at[p, 1])
                        arrived(piece(over, p)[1], ssem_y.at[p, 2])

    def inverse_of(n):
        if n < 8:
            return linv.at[sub, n]
        if n < 12:
            return tlinv.at[n - 8]
        if n < 16:
            return tuinv.at[15 - n]
        return uinv.at[sub, 23 - n]

    def send_inverse(n):
        for d in (1, 2, 3):
            remote(inverse_of(n), inv.at[n, row], ssem_i.at[n, d - 1], rsem_i.at[n, d], zpeer(d)).start()
        pltpu.make_async_copy(inverse_of(n), inv.at[n, row], rsem_i.at[n, 0]).start()

    def prepare_inverse(n):
        for d in range(4):
            arrived(inv.at[0, 0], rsem_i.at[n, d])
        whole = inv[n].reshape(256, 256).T
        invh[n % 2], invl[n % 2] = halves(whole)

    def sub_block(i, k):
        return slab[k // 2, i, :, (k % 2) * 256 : (k % 2) * 256 + 256]

    def terms(n):
        if n < 8:
            return [(lambda k=k: sub_block(n, k), k) for k in range(n)]
        if n < 12:
            return [(lambda u=u: tops[u, n - 8], 8 + u) for u in range(n - 8)]
        if n < 16:
            t = 15 - n
            return [(lambda u=u: tops[u, t], 15 - u) for u in range(3, t, -1)]
        i = 23 - n
        return [(lambda k=k: sub_block(i, k), 23 - k) for k in range(7, i, -1)]

    def apply(block, n):
        return product(halves(block()), (solh[n], soll[n]))

    def base_of(n):
        if n < 8:
            return base[n]
        if n < 12:
            return trhs[pl.ds((n - 8) * 4, 4)].reshape(64, 128)
        if n < 16:
            return sol[23 - n, rows]
        return sol[23 - n, rows] - coup[23 - n]

    def before(n):
        value = base_of(n)
        for block, k in terms(n):
            if k != n - 1:
                value = value - apply(block, k)
        return value

    def finish(n, value):
        for block, k in terms(n):
            if k == n - 1:
                value = value - apply(block, k)
        return value

    def start_gather(n, value):
        gath[n, rows] = value
        for d in (1, 2, 3):
            remote(gath.at[n, rows], gath.at[n, rows], ssem_g.at[n, d - 1], rsem_g.at[n, d - 1], zpeer(d)).start()

    def solve(n):
        for d in (1, 2, 3):
            arrived(gath.at[0, pl.ds(0, 64)], rsem_g.at[n, d - 1])
        value = product((invh[n % 2], invl[n % 2]), halves(gath[n]))
        sol[n] = value
        solh[n], soll[n] = halves(value)

    def mask(t):
        return present_ref[t, sub].astype(F32)

    def contrib(owner):
        pair = (
            jnp.concatenate([solh[2 * owner], solh[2 * owner + 1]], axis=0),
            jnp.concatenate([soll[2 * owner], soll[2 * owner + 1]], axis=0),
        )
        for t in range(4):
            value = product(halves(lowers[owner, t]), pair) * mask(t)
            part[pl.ds(4 * t, 4)] += value.reshape(4, 16, 128)

    def couple(t, first, last):
        value = product(halves(uppers[t, first:last].reshape((last - first) * 64, 256)), (solh[15 - t], soll[15 - t]))
        return (value * mask(t)).reshape(last - first, 64, 128)

    base_copy = pltpu.make_async_copy(
        rhs.at[sub, :, :, pl.ds(pl.multiple_of(half * 128, 128), 128)], base, misc.at[0]
    )
    base_copy.start()
    send_inverse(0)
    travel(first=True, sends=SEND_AT[-1])
    send_inverse(1)
    quarter = lax.broadcasted_iota(jnp.int32, (256, 128), 1) // 32
    narrow = toprhs[...].reshape(256, 32)
    spread = jnp.concatenate([narrow] * 4, axis=1)
    here = jnp.where(jnp.logical_and(leaf // 4 == half, sub == 0), lax.rem(leaf, 4), -1)
    part[...] = -jnp.where(quarter == here, spread, 0.0).reshape(16, 16, 128)
    base_copy.wait()
    carried = base_of(0)

    for n in range(24):
        if n == 8:
            contrib(3)
            travel(arrivals=(9, 10))
            contrib(0)
            me = sub * 8 + leaf
            red[pl.ds(me, 1)] = part[pl.ds(me, 1)]
            for k, (o, d) in enumerate(group):
                peer, m = member(o, d)
                remote(part.at[m], red.at[me], ssem_r.at[k], rsem_r.at[k], peer).start()
            for k in range(15):
                arrived(red.at[0], rsem_r.at[k])
            total = red[0]
            for m in range(1, 16):
                total = total + red[m]
            trhs[pl.ds(me, 1)] = -total[None]
            for k, (o, d) in enumerate(group):
                peer, m = member(o, d)
                remote(trhs.at[me], trhs.at[me], ssem_a.at[k], rsem_a.at[k], peer).start()
            for k in range(15):
                arrived(trhs.at[0], rsem_a.at[k])
            carried = base_of(8)
        if n == 12:
            value = sol[11, rows]
        elif n == 16:
            value = sol[7, rows] - coup[7] - couple(0, 7, 8)[0]
        else:
            value = finish(n, carried)
        start_gather(n, value)
        if n + 2 < 24:
            send_inverse(n + 2)
        travel(sends=SEND_AT.get(n, ()), relays=RELAY_AT.get(n, ()))
        prepare_inverse(n)
        travel(arrivals=ARRIVE_AT.get(n, ()))
        if n == 7:
            contrib(2)
        if n == 16:
            coup[0:7] += couple(0, 0, 7)
            for o in range(4):

                @pl.when(col == o)
                def _():
                    remote(sol.at[15 - (o ^ 1)], swap, ssem_x.at[0], rsem_x.at[0], ypeer(o ^ 1)).start()

        if n == 14:
            coup[...] = couple(3, 0, 8) + couple(2, 0, 8)
        if n == 15:
            coup[...] += couple(1, 0, 8)
        if n + 1 not in (8, 12, 16, 24):
            carried = before(n + 1)
        if n == 7:
            contrib(1)
        solve(n)
        if n >= 16:
            i = 23 - n
            o = i // 2
            place = sub_out.at[0, sub, i % 2, :, pl.ds(pl.multiple_of(half * 128, 128), 128)]

            @pl.when(col == o)
            def _():
                pltpu.make_async_copy(sol.at[n], place, rsem_o.at[i % 2, col]).start()

            @pl.when(col != o)
            def _():
                remote(sol.at[n], place, ssem_o.at[i], rsem_o.at[i % 2, col], ypeer(o)).start()

    arrived(swap, rsem_x.at[0])
    top = jnp.where(leaf // 4 == half, sol[15 - col], swap[...])
    q = lax.rem(leaf, 4)
    picked = top[:, 0:32]
    for k in range(1, 4):
        picked = jnp.where(q == k, top[:, 32 * k : 32 * k + 32], picked)
    top_out[0] = picked

    travel(last=True)
    for n in range(24):
        for d in range(3):
            arrived(inv.at[0, 0], ssem_i.at[n, d])
            arrived(gath.at[0, pl.ds(0, 64)], ssem_g.at[n, d])
    for k in range(15):
        arrived(red.at[0], ssem_r.at[k])
        arrived(red.at[0], ssem_a.at[k])
    arrived(swap, ssem_x.at[0])
    for i in range(8):

        @pl.when(col != i // 2)
        def _():
            arrived(sol.at[0], ssem_o.at[i])

    for k in range(2):
        for c in range(4):
            arrived(sol.at[0], rsem_o.at[k, c])


def per_device(
    subtree_factor, sub_linv, sub_uinv, lower_panel, upper_panel, panel_rows, upper_level_factor, top_linv, top_uinv, sub_rhs, top_rhs
):
    anywhere = pl.BlockSpec(memory_space=pl.ANY)
    vmem = pl.BlockSpec(memory_space=pltpu.VMEM)
    dma = pltpu.SemaphoreType.DMA
    return pl.pallas_call(
        kernel,
        name="solve",
        out_shape=(
            jax.ShapeDtypeStruct((1, 2, 2, 256, 256), F32),
            jax.ShapeDtypeStruct((1, 256, 32), F32),
        ),
        in_specs=[pl.BlockSpec(memory_space=pltpu.SMEM)] + [anywhere] * 9 + [vmem],
        out_specs=(anywhere, vmem),
        scratch_shapes=[
            pltpu.VMEM((4, 8, 64, 512), F32),
            pltpu.VMEM((4, 4, 64, 512), F32),
            pltpu.VMEM((4, 8, 64, 256), F32),
            pltpu.VMEM((4, 4, 64, 256), F32),
            pltpu.VMEM((24, 4, 64, 256), F32),
            pltpu.VMEM((8, 64, 128), F32),
            pltpu.VMEM((24, 256, 128), F32),
            pltpu.VMEM((24, 256, 128), F32),
            pltpu.VMEM((24, 256, 128), BF16),
            pltpu.VMEM((24, 256, 128), BF16),
            pltpu.VMEM((2, 256, 256), BF16),
            pltpu.VMEM((2, 256, 256), BF16),
            pltpu.VMEM((8, 64, 128), F32),
            pltpu.VMEM((16, 16, 128), F32),
            pltpu.VMEM((16, 16, 128), F32),
            pltpu.VMEM((16, 16, 128), F32),
            pltpu.VMEM((256, 128), F32),
            dma((NPOS, 3)),
            dma((NPOS, 4)),
            dma((24, 3)),
            dma((24, 4)),
            dma((24, 3)),
            dma((24, 3)),
            dma((15,)),
            dma((15,)),
            dma((15,)),
            dma((15,)),
            dma((8,)),
            dma((2, 4)),
            dma((1,)),
            dma((1,)),
            dma((1,)),
        ],
        compiler_params=pltpu.CompilerParams(collective_id=0, has_side_effects=True, vmem_limit_bytes=56 << 20),
    )(
        panel_rows[0],
        subtree_factor[0],
        sub_linv[0],
        sub_uinv[0],
        jnp.transpose(lower_panel[0], (2, 0, 1, 3)),
        upper_panel[0],
        upper_level_factor,
        top_linv,
        top_uinv,
        sub_rhs[0],
        top_rhs,
    )


def solution(mesh):
    placed = (
        P("leaf", None, None, "prow", "pcol"),
        P("leaf", None, None, "prow", None),
        P("leaf", None, None, "prow", None),
        P("leaf", None, "prow", None, "pcol"),
        P("leaf", None, None, "prow", "pcol"),
        P("leaf", None, None),
        P(None, "prow", "pcol"),
        P(None, "prow", None),
        P(None, "prow", None),
        P("leaf", None, None, "prow", None),
        P(None, "prow", "leaf"),
    )
    return jax.shard_map(
        per_device,
        mesh=mesh,
        in_specs=placed,
        out_specs=(P("leaf", None, "pcol", None, None), P("pcol", None, "leaf")),
        check_vma=False,
    )
```

time: 2310 us -> 192 us (0.08)
  waiting for transfers between devices: 2070 us -> 0 us
  Pallas kernels: 0 us -> 182 us
  local copies, waits for them, and re-layouts: 108 us -> 9.2 us
  matrix products: 93 us -> 0 us
    psum x25 -> x0, waiting for transfers between devices: 2070 us -> none  [the longest x24 2020 us: sweep_blocks(): block_value = lax.psum(inverse_part, ('prow', 'pcol'))]
    pallas_call x0 -> x1, Pallas kernels: none -> 182 us  [per_device(): pl.pallas_call(kernel, name='solve', out_shape=(jax.ShapeDtypeStruct((1,...]
    dot_general x48 -> x0, matrix products: 93 us -> none  [the longest x24 53.3 us: sweep_blocks(): jnp.einsum('gab,gar->gbr', inverses[:, sweep_step_index], local_side, pre...]
    dynamic_slice x36 -> x0, local copies, waits for them, and re-layouts: 51.5 us -> none  [the longest x28 43.2 us: sweep_blocks(): lax.dynamic_slice_in_dim(solved, owned_start, owned_count, 1)]
    scatter x24 -> x0, local copies, waits for them, and re-layouts: 47.2 us -> none  [sweep_blocks(): solved = solved.at[:, sweep_step_index].set(block_value)]
  transfers between devices with their start and end apart: 25 -> 0, of which waited for: 25 -> 0; matrix products, arithmetic and copies ran while one was open for 1% -> 0% of each run, Pallas kernels for 0% -> 0%
where the time goes in v1:
time: 192 us; the launch traced here: 191 us
  Pallas kernels  182 us (95%)
  local copies, waits for them, and re-layouts  9.2 us (5%)
    pallas_call x1, Pallas kernels, per_device(): pl.pallas_call(kernel, name='solve', out_shape=(jax.ShapeDtypeStruct((1,...  182 us
    unnamed x3, local copies, waits for them, and re-layouts  6.27 us

profile of v1, /device:TPU:0, one launch (start us, length us, event | category | flops | bytes accessed | tf_op | source)
XLA Modules:
  0.0 191.4 jit_solution(8085056176815214385)
XLA Ops:
  0.6 1.3 copy.14.present_ref
  2.0 1.6 copy.15.toprhs
  3.6 2.4 %copy.18 = f32[1,4,64,2,512]{4,2,1,3,0:T(8,128)} copy(f32[1,4,64,2,512]{4,3,2,1,0:T(2,128)} %param.14) | data formatting | bytes 2097152 | tf_op args[3]
  6.0 181.5 %solve.1 = (f32[1,2,2,256,256]{4,3,2,1,0:T(8,128)}, f32[1,256,32]{2,1,0:T(8,128)}) custom-call(s32[4,2]{1,0:T(4,128)} %copy.14.present_ref, f32[2,8,64,512]{3,2,1,0:T(8,128)} %bitcast.12, f32[2,8,64,256]{3,2,1,0:T(8,128)} %bitcast.13, f32[2,8,64,256]{3,2,1,0:T(8,128)} %bitcast.14, f32[2,4,64,512]{3,2,1,0:T(8,128)} %bitcast.11, f32[2,8,64,256]{3,2,1,0:T(8,128)} %bitcast.15, ...), custom_call_target="tpu_custom_call" | custom-call | tf_op jit(solution)/shard_map/solve/pallas_call | solution.py:366
  187.5 1.6 copy.16
  189.1 2.3 %copy.20 = f32[1,2,2,256,256]{4,3,2,1,0:T(8,128)} copy(f32[1,2,2,256,256]{4,3,2,1,0:T(8,128)} %get-tuple-element.6) | data formatting | bytes 2097152

commit v2 on v1

v2 whole, which is shorter than its diff:
```python
import jax
import jax.numpy as jnp
from jax import lax
from jax.experimental import pallas as pl
from jax.experimental.pallas import tpu as pltpu
from jax.sharding import PartitionSpec as P

MESH = pl.DeviceIdType.MESH
F32 = jnp.float32
BF16 = jnp.bfloat16
NPOS = 22
SEND_AT = {-1: (0, 1, 2), 0: (3,), 1: (4,), 2: (5,), 3: (6,), 4: (7, 8), 5: (9,), 6: (10,), 7: (11,), "sum": (12,), "share": (13, 14), 8: (16,), 9: (17,), 10: (18,), 11: (19,), 12: (20,), 13: (21,), "top": (15,)}
RELAY_AT = {0: (0, 1), 1: (2,), 2: (3,), 3: (4,), 4: (5,), 5: (6, 7), 6: (8,), 7: (9, 10), "share": (11, 12), "top": (13, 14), 8: (15,), 9: (16,), 10: (17,), 11: (18,), 12: (19,), 13: (20,), 14: (21,)}
ARRIVE_AT = {0: (0,), 1: (1,), 2: (2,), 3: (3,), 4: (4,), 5: (5,), 6: (6,), 7: (7, 8), "end": (9, 10), "top": (11, 12, 13, 14), 8: (15,), 9: (16,), 10: (17,), 11: (18,), 12: (19,), 13: (20,), 14: (21,)}


def halves(value):
    high = value.astype(BF16)
    return high, (value - high.astype(F32)).astype(BF16)


def product(left, right):
    def one(a, b):
        return jnp.dot(a, b, preferred_element_type=F32)

    return one(left[0], right[0]) + (one(left[0], right[1]) + one(left[1], right[0]))


def kernel(
    present_ref,
    factor,
    linv,
    uinv,
    lower,
    upper,
    topf,
    tlinv,
    tuinv,
    rhs,
    toprhs,
    sub_out,
    top_out,
    slab,
    lowers,
    uppers,
    tops,
    inv,
    base,
    gath,
    sol,
    solh,
    soll,
    invh,
    invl,
    coup,
    part,
    red,
    trhs,
    swap,
    blockh,
    blockl,
    tsol,
    tsolh,
    tsoll,
    ssem_y,
    rsem_y,
    ssem_i,
    rsem_i,
    ssem_g,
    rsem_g,
    ssem_r,
    rsem_r,
    ssem_a,
    rsem_a,
    ssem_o,
    rsem_o,
    misc,
    ssem_x,
    rsem_x,
    ssem_t,
    rsem_t,
    ssem_v,
    rsem_v,
    ssem_w,
    rsem_w,
    ssem_p,
    rsem_p,
    ssem_q,
    rsem_q,
):
    leaf = lax.axis_index("leaf")
    row = lax.axis_index("prow")
    col = lax.axis_index("pcol")
    sub = col // 2
    half = lax.rem(col + sub, 2)
    beside = col + 1 - 2 * lax.rem(col, 2)
    across = 3 - col
    rows = pl.ds(pl.multiple_of(row * 64, 64), 64)

    def zpeer(d):
        return (leaf, lax.rem(row + d, 4), col)

    def ypeer(c):
        return (leaf, row, c)

    group = []
    for other in (0, 1):
        for d in range(8):
            if other or d:
                group.append((other, d))

    def member(other, d):
        there = lax.rem(leaf + d, 8)
        return (there, row, across if other else col), (1 - sub if other else sub) * 8 + there

    core = lax.rem(leaf, 2)
    mine_t = leaf // 2
    partner = (leaf + 1 - 2 * core, row, col)
    wide = []
    for other in (0, 1):
        for dx in range(4):
            for dr in range(4):
                if other or dx or dr:
                    wide.append((lax.rem(leaf + 2 * dx, 8), lax.rem(row + dr, 4), across if other else col))

    def xpeer(d):
        return (lax.rem(leaf + 2 * d, 8), row, col)

    barrier = pltpu.get_barrier_semaphore()
    greeted = wide + [ypeer(beside), ypeer(3 - beside)]
    greeted += [member(o, d)[0] for o, d in group if d % 2]
    for peer in greeted:
        pl.semaphore_signal(barrier, inc=1, device_id=peer, device_id_type=MESH)
    pl.semaphore_wait(barrier, len(greeted))

    def remote(src, dst, send, recv, peer):
        return pltpu.make_async_remote_copy(
            src_ref=src, dst_ref=dst, send_sem=send, recv_sem=recv, device_id=peer, device_id_type=MESH
        )

    def arrived(ref, sem):
        pltpu.make_async_copy(ref, ref, sem).wait()

    def piece(owner, p):
        near = 7 - 2 * owner
        if p < near:
            i = 2 * owner + 1 + p
            if p == 0:
                return lambda s: factor.at[s, i, :, pl.ds(0, 256)], slab.at[owner, i, :, pl.ds(0, 256)]
            return lambda s: factor.at[s, i], slab.at[owner, i]
        if p < near + 4:
            t = p - near
            return lambda s: lower.at[t, :, s], lowers.at[owner, t]
        if p < 11:
            return None
        if p < 15:
            i = pl.ds(2 * (p - 11), 2)
            return lambda s: upper.at[s, i], uppers.at[owner, i]
        i = 21 - p
        if i > 2 * owner:
            return None
        if i == 2 * owner:
            return lambda s: factor.at[s, i, :, pl.ds(256, 256)], slab.at[owner, i, :, pl.ds(256, 256)]
        return lambda s: factor.at[s, i], slab.at[owner, i]

    def travel(sends=(), relays=(), arrivals=(), first=False, last=False):
        for o in range(4):
            mine, there, over = o // 2, 1 - o // 2, 3 - o

            @pl.when(col == o)
            def _():
                if first:
                    for p in range(NPOS):
                        if piece(o, p):
                            src, dst = piece(o, p)
                            pltpu.make_async_copy(src(mine), dst, rsem_y.at[p, o]).start()
                for p in sends:
                    if piece(o, p):
                        src, dst = piece(o, p)
                        remote(src(mine), dst, ssem_y.at[p, 0], rsem_y.at[p, o], ypeer(o ^ 1)).start()
                        remote(src(there), dst, ssem_y.at[p, 1], rsem_y.at[p, o], ypeer(over)).start()
                for p in relays:
                    if piece(over, p):
                        dst = piece(over, p)[1]
                        arrived(dst, rsem_y.at[p, over])
                        remote(dst, dst, ssem_y.at[p, 2], rsem_y.at[p, over], ypeer(o ^ 1)).start()
                for p in arrivals:
                    for other in (o, o ^ 1, 3 - (o ^ 1)):
                        if piece(other, p):
                            arrived(piece(other, p)[1], rsem_y.at[p, other])
                if last:
                    for p in range(NPOS):
                        if piece(o, p):
                            dst = piece(o, p)[1]
                            arrived(dst, ssem_y.at[p, 0])
                            arrived(dst, ssem_y.at[p, 1])
                        if piece(over, p):
                            arrived(piece(over, p)[1], ssem_y.at[p, 2])

    def at(point):
        travel(SEND_AT.get(point, ()), RELAY_AT.get(point, ()), ARRIVE_AT.get(point, ()))

    my_rows = pl.ds(pl.multiple_of(core * 32, 32), 32)

    def collect_top():
        for d in (1, 2, 3):
            remote(topf.at[mine_t, my_rows], tops.at[mine_t, core, col, row], ssem_t.at[d - 1], rsem_t.at[d], ypeer(lax.rem(col + d, 4))).start()
        pltpu.make_async_copy(topf.at[mine_t, my_rows], tops.at[mine_t, core, col, row], rsem_t.at[0]).start()
        for k, src in ((0, tlinv), (1, tuinv)):
            for d in (1, 2, 3):
                remote(src.at[mine_t, my_rows], tops.at[mine_t, core, 4 + k, row], ssem_v.at[k, d - 1], rsem_v.at[k, d], zpeer(d)).start()
            pltpu.make_async_copy(src.at[mine_t, my_rows], tops.at[mine_t, core, 4 + k, row], rsem_v.at[k, 0]).start()

    def collect_rows():
        for d in range(4):
            arrived(tops.at[0, 0, 0, 0], rsem_t.at[d])
        ref = tops.at[mine_t, core, pl.ds(0, 4), row]
        for d in (1, 2, 3):
            remote(ref, ref, ssem_v.at[2, d - 1], rsem_v.at[2, d], zpeer(d)).start()

    def share_top():
        for d in range(4):
            arrived(tops.at[0, 0, 0, 0], rsem_v.at[0, d])
            arrived(tops.at[0, 0, 0, 0], rsem_v.at[1, d])
        for d in (1, 2, 3):
            arrived(tops.at[0, 0, pl.ds(0, 4), 0], rsem_v.at[2, d])
        ref = tops.at[mine_t, core]
        for d in (1, 3, 2):
            remote(ref, ref, ssem_w.at[d - 1], rsem_w.at[d - 1], xpeer(d)).start()
        remote(ref, ref, ssem_p.at[0], rsem_p.at[0], partner).start()

    def hand_top(d):
        arrived(tops.at[0, 0], rsem_w.at[d - 1])
        ref = tops.at[lax.rem(mine_t + 4 - d, 4), core]
        remote(ref, ref, ssem_p.at[d], rsem_p.at[d], partner).start()

    def top_block(t, u):
        return jnp.concatenate([tops[t, h, u, r] for r in range(4) for h in range(2)], axis=0)

    def prepare_top():
        for d in range(4):
            arrived(tops.at[0, 0], rsem_p.at[d])
        for t in range(4):
            for u in range(4):
                if t != u:
                    blockh[4 * t + u], blockl[4 * t + u] = halves(top_block(t, u))
            for k in range(2):
                blockh[16 + 2 * t + k], blockl[16 + 2 * t + k] = halves(top_block(t, 4 + k).T)

    def top_product(b, k):
        return product((blockh[b], blockl[b]), (tsolh[k], tsoll[k]))

    def top_rhs_of(t):
        parts = []
        for r in range(4):
            for j in range(4):
                m = 4 * t + j
                parts.append(trhs[m % 2, r, (m // 8) * 4 + (m % 8) // 2])
        return jnp.concatenate(parts, axis=0)

    def solve_top():
        for t in range(4):
            value = top_rhs_of(t)
            for u in range(t):
                value = value - top_product(4 * t + u, u)
            value = product((blockh[16 + 2 * t], blockl[16 + 2 * t]), halves(value))
            tsol[t] = value
            tsolh[t], tsoll[t] = halves(value)
        for t in (3, 2, 1, 0):
            value = tsol[t]
            for u in range(3, t, -1):
                value = value - top_product(4 * t + u, u)
            value = product((blockh[17 + 2 * t], blockl[17 + 2 * t]), halves(value))
            tsol[t] = value
            tsolh[t], tsoll[t] = halves(value)

    def inverse_of(n):
        return linv.at[sub, n] if n < 8 else uinv.at[sub, 15 - n]

    def send_inverse(n):
        for d in (1, 2, 3):
            remote(inverse_of(n), inv.at[n, row], ssem_i.at[n, d - 1], rsem_i.at[n, d], zpeer(d)).start()
        pltpu.make_async_copy(inverse_of(n), inv.at[n, row], rsem_i.at[n, 0]).start()

    def prepare_inverse(n):
        for d in range(4):
            arrived(inv.at[0, 0], rsem_i.at[n, d])
        whole = inv[n].reshape(256, 256).T
        invh[n % 2], invl[n % 2] = halves(whole)

    def sub_block(i, k):
        return slab[k // 2, i, :, (k % 2) * 256 : (k % 2) * 256 + 256]

    def terms(n):
        if n < 8:
            return [(lambda k=k: sub_block(n, k), k) for k in range(n)]
        i = 15 - n
        return [(lambda k=k: sub_block(i, k), 15 - k) for k in range(7, i, -1)]

    def apply(block, n):
        return product(halves(block()), (solh[n], soll[n]))

    def base_of(n):
        if n < 8:
            return base[n]
        return sol[15 - n, rows] - coup[15 - n]

    def before(n):
        value = base_of(n)
        for block, k in terms(n):
            if k != n - 1:
                value = value - apply(block, k)
        return value

    def finish(n, value):
        for block, k in terms(n):
            if k == n - 1:
                value = value - apply(block, k)
        return value

    def start_gather(n, value):
        gath[n, rows] = value
        for d in (1, 2, 3):
            remote(gath.at[n, rows], gath.at[n, rows], ssem_g.at[n, d - 1], rsem_g.at[n, d - 1], zpeer(d)).start()

    def solve(n):
        for d in (1, 2, 3):
            arrived(gath.at[0, pl.ds(0, 64)], rsem_g.at[n, d - 1])
        value = product((invh[n % 2], invl[n % 2]), halves(gath[n]))
        sol[n] = value
        solh[n], soll[n] = halves(value)

    def mask(t):
        return present_ref[sub, t].astype(F32)

    def contrib(owner):
        pair = (
            jnp.concatenate([solh[2 * owner], solh[2 * owner + 1]], axis=0),
            jnp.concatenate([soll[2 * owner], soll[2 * owner + 1]], axis=0),
        )
        for t in range(4):
            value = product(halves(lowers[owner, t]), pair) * mask(t)
            part[pl.ds(4 * t, 4)] += value.reshape(4, 16, 128)

    def couple(first, last):
        total = None
        for t in range(4):
            value = product(halves(uppers[t, first:last].reshape((last - first) * 64, 256)), (tsolh[t], tsoll[t])) * mask(t)
            total = value if total is None else total + value
        return total.reshape(last - first, 64, 128)

    base_copy = pltpu.make_async_copy(
        rhs.at[sub, :, :, pl.ds(pl.multiple_of(half * 128, 128), 128)], base, misc.at[0]
    )
    base_copy.start()
    send_inverse(0)
    travel(first=True, sends=SEND_AT[-1])
    collect_top()
    send_inverse(1)
    quarter = lax.broadcasted_iota(jnp.int32, (256, 128), 1) // 32
    narrow = jnp.concatenate([toprhs[t].T for t in range(4)], axis=0)
    spread = jnp.concatenate([narrow] * 4, axis=1)
    here = jnp.where(jnp.logical_and(leaf // 4 == half, sub == 0), lax.rem(leaf, 4), -1)
    part[...] = -jnp.where(quarter == here, spread, 0.0).reshape(16, 16, 128)
    base_copy.wait()
    carried = base_of(0)

    for n in range(16):
        if n == 8:
            contrib(3)
            at("end")
            contrib(0)
            me = sub * 8 + leaf
            red[pl.ds(me, 1)] = part[pl.ds(me, 1)]
            for k, (o, d) in enumerate(group):
                peer, m = member(o, d)
                remote(part.at[m], red.at[me], ssem_r.at[k], rsem_r.at[k], peer).start()
            at("sum")
            hand_top(1)
            hand_top(3)
            for k in range(15):
                arrived(red.at[0], rsem_r.at[k])
            total = red[0]
            for m in range(1, 16):
                total = total + red[m]
            slot = sub * 4 + mine_t
            trhs[core, row, pl.ds(slot, 1)] = -total[None]
            ref = trhs.at[core, row, slot]
            for k, peer in enumerate(wide):
                remote(ref, ref, ssem_a.at[k], rsem_a.at[k], peer).start()
            hand_top(2)
            at("share")
            prepare_top()
            for k in range(31):
                arrived(red.at[0], rsem_a.at[k])
            remote(trhs.at[core], trhs.at[core], ssem_q.at[0], rsem_q.at[0], partner).start()
            arrived(trhs.at[0], rsem_q.at[0])
            solve_top()
            for o in range(4):

                @pl.when(col == o)
                def _():
                    remote(tsol.at[o ^ 1], swap, ssem_x.at[0], rsem_x.at[0], ypeer(o ^ 1)).start()

            at("top")
            value = sol[7, rows] - couple(7, 8)[0]
        else:
            value = finish(n, carried)
        start_gather(n, value)
        if n + 2 < 16:
            send_inverse(n + 2)
        travel(sends=SEND_AT.get(n, ()), relays=RELAY_AT.get(n, ()))
        prepare_inverse(n)
        if n == 0:
            collect_rows()
        if n == 1:
            share_top()
        travel(arrivals=ARRIVE_AT.get(n, ()))
        if n == 7:
            contrib(2)
        if n == 8:
            coup[0:7] = couple(0, 7)
        if n + 1 not in (8, 16):
            carried = before(n + 1)
        if n == 7:
            contrib(1)
        solve(n)
        if n >= 8:
            i = 15 - n
            o = i // 2
            place = sub_out.at[0, sub, i % 2, :, pl.ds(pl.multiple_of(half * 128, 128), 128)]

            @pl.when(col == o)
            def _():
                pltpu.make_async_copy(sol.at[n], place, rsem_o.at[i % 2, col]).start()

            @pl.when(col != o)
            def _():
                remote(sol.at[n], place, ssem_o.at[i], rsem_o.at[i % 2, col], ypeer(o)).start()

    arrived(swap, rsem_x.at[0])
    top = jnp.where(leaf // 4 == half, tsol[col], swap[...])
    q = lax.rem(leaf, 4)
    picked = top[:, 0:32]
    for k in range(1, 4):
        picked = jnp.where(q == k, top[:, 32 * k : 32 * k + 32], picked)
    top_out[0] = picked.T

    travel(last=True)
    for n in range(16):
        for d in range(3):
            arrived(inv.at[0, 0], ssem_i.at[n, d])
            arrived(gath.at[0, pl.ds(0, 64)], ssem_g.at[n, d])
    for k in range(15):
        arrived(red.at[0], ssem_r.at[k])
    for k in range(31):
        arrived(red.at[0], ssem_a.at[k])
    for d in range(3):
        arrived(tops.at[0, 0, 0, 0], ssem_t.at[d])
        arrived(tops.at[0, 0, 0, 0], ssem_v.at[0, d])
        arrived(tops.at[0, 0, 0, 0], ssem_v.at[1, d])
        arrived(tops.at[0, 0, pl.ds(0, 4), 0], ssem_v.at[2, d])
        arrived(tops.at[0, 0], ssem_w.at[d])
    for d in range(4):
        arrived(tops.at[0, 0], ssem_p.at[d])
    arrived(trhs.at[0], ssem_q.at[0])
    arrived(swap, ssem_x.at[0])
    for i in range(8):

        @pl.when(col != i // 2)
        def _():
            arrived(sol.at[0], ssem_o.at[i])

    for k in range(2):
        for c in range(4):
            arrived(sol.at[0], rsem_o.at[k, c])


def per_device(
    subtree_factor, sub_linv, sub_uinv, lower_panel, upper_panel, panel_rows, upper_level_factor, top_linv, top_uinv, sub_rhs, top_rhs
):
    anywhere = pl.BlockSpec(memory_space=pl.ANY)
    vmem = pl.BlockSpec(memory_space=pltpu.VMEM)
    dma = pltpu.SemaphoreType.DMA
    solved, top = pl.pallas_call(
        kernel,
        name="solve",
        out_shape=(
            jax.ShapeDtypeStruct((1, 2, 2, 256, 256), F32),
            jax.ShapeDtypeStruct((1, 32, 256), F32),
        ),
        in_specs=[pl.BlockSpec(memory_space=pltpu.SMEM)] + [anywhere] * 9 + [vmem],
        out_specs=(anywhere, vmem),
        scratch_shapes=[
            pltpu.VMEM((4, 8, 64, 512), F32),
            pltpu.VMEM((4, 4, 64, 512), F32),
            pltpu.VMEM((4, 8, 64, 256), F32),
            pltpu.VMEM((4, 2, 6, 4, 32, 256), F32),
            pltpu.VMEM((16, 4, 64, 256), F32),
            pltpu.VMEM((8, 64, 128), F32),
            pltpu.VMEM((16, 256, 128), F32),
            pltpu.VMEM((16, 256, 128), F32),
            pltpu.VMEM((16, 256, 128), BF16),
            pltpu.VMEM((16, 256, 128), BF16),
            pltpu.VMEM((2, 256, 256), BF16),
            pltpu.VMEM((2, 256, 256), BF16),
            pltpu.VMEM((8, 64, 128), F32),
            pltpu.VMEM((16, 16, 128), F32),
            pltpu.VMEM((16, 16, 128), F32),
            pltpu.VMEM((2, 4, 8, 16, 128), F32),
            pltpu.VMEM((256, 128), F32),
            pltpu.VMEM((24, 256, 256), BF16),
            pltpu.VMEM((24, 256, 256), BF16),
            pltpu.VMEM((4, 256, 128), F32),
            pltpu.VMEM((4, 256, 128), BF16),
            pltpu.VMEM((4, 256, 128), BF16),
            dma((NPOS, 3)),
            dma((NPOS, 4)),
            dma((16, 3)),
            dma((16, 4)),
            dma((16, 3)),
            dma((16, 3)),
            dma((15,)),
            dma((15,)),
            dma((31,)),
            dma((31,)),
            dma((8,)),
            dma((2, 4)),
            dma((1,)),
            dma((1,)),
            dma((1,)),
            dma((3,)),
            dma((4,)),
            dma((3, 3)),
            dma((3, 4)),
            dma((3,)),
            dma((3,)),
            dma((4,)),
            dma((4,)),
            dma((1,)),
            dma((1,)),
        ],
        compiler_params=pltpu.CompilerParams(collective_id=0, has_side_effects=True, vmem_limit_bytes=56 << 20),
    )(
        jnp.transpose(panel_rows[0]),
        subtree_factor[0],
        sub_linv[0],
        sub_uinv[0],
        lower_panel[0],
        upper_panel[0],
        upper_level_factor,
        top_linv,
        top_uinv,
        sub_rhs[0],
        jnp.swapaxes(top_rhs, 1, 2),
    )
    return solved, jnp.swapaxes(top, 1, 2)


def solution(mesh):
    placed = (
        P("leaf", None, None, "prow", "pcol"),
        P("leaf", None, None, "prow", None),
        P("leaf", None, None, "prow", None),
        P("leaf", None, "prow", None, "pcol"),
        P("leaf", None, None, "prow", "pcol"),
        P("leaf", None, None),
        P(None, "prow", "pcol"),
        P(None, "prow", None),
        P(None, "prow", None),
        P("leaf", None, None, "prow", None),
        P(None, "prow", "leaf"),
    )
    return jax.shard_map(
        per_device,
        mesh=mesh,
        in_specs=placed,
        out_specs=(P("leaf", None, "pcol", None, None), P("pcol", None, "leaf")),
        check_vma=False,
    )
```

time: 192 us -> 158 us (0.82)
  Pallas kernels: 182 us -> 154 us
  local copies, waits for them, and re-layouts: 9.2 us -> 2.91 us
    pallas_call x1, Pallas kernels: 182 us -> 154 us  [per_device(): pl.pallas_call(kernel, name='solve', out_shape=(jax.ShapeDtypeStruct((1,...]
    unnamed x3 -> x4, local copies, waits for them, and re-layouts: 6.27 us -> 2.91 us
where the time goes in v2:
time: 158 us
  Pallas kernels  154 us (97%)
  local copies, waits for them, and re-layouts  2.91 us (2%)
    pallas_call x1, Pallas kernels, per_device(): pl.pallas_call(kernel, name='solve', out_shape=(jax.ShapeDtypeStruct((1,...  154 us

profile of v2, /device:TPU:0, one launch (start us, length us, event | category | flops | bytes accessed | tf_op | source)
XLA Modules:
  0.0 157.9 jit_solution(15662220845075338758)
XLA Ops:
  0.6 154.3 %solve.1 = (f32[1,2,2,256,256]{4,3,2,1,0:T(8,128)}, f32[1,32,256]{2,1,0:T(8,128)}) custom-call(s32[2,4]{1,0:T(2,128)} %bitcast.19, f32[2,8,64,512]{3,2,1,0:T(8,128)} %bitcast.11, f32[2,8,64,256]{3,2,1,0:T(8,128)} %bitcast.12, f32[2,8,64,256]{3,2,1,0:T(8,128)} %bitcast.13, f32[4,64,2,512]{3,2,1,0:T(2,128)} %bitcast.14, f32[2,8,64,256]{3,2,1,0:T(8,128)} %bitcast.15, ...), custom_call_target="tpu_custom_call" | custom-call | tf_op jit(solution)/shard_map/solve/pallas_call | solution.py:485
  155.0 0.0 copy-start
  155.0 2.3 %copy.15 = f32[1,2,2,256,256]{4,3,2,1,0:T(8,128)} copy(f32[1,2,2,256,256]{4,3,2,1,0:T(8,128)} %get-tuple-element.8) | data formatting | bytes 2097152
  157.3 0.0 copy-done
  157.3 0.6 copy.16
Async XLA Ops:
  155.0 2.3 %copy-start = (f32[1,32,256]{2,1,0:T(8,128)S(1)}, f32[1,32,256]{2,1,0:T(8,128)}, u32[]{:S(2)}) copy-start(f32[1,32,256]{2,1,0:T(8,128)} %get-tuple-element.5) | copy-start | bytes 98308

commit v3 on v2

--- a/solution.py
+++ b/solution.py
@@ -9,9 +9,9 @@
 F32 = jnp.float32
 BF16 = jnp.bfloat16
 NPOS = 22
-SEND_AT = {-1: (0, 1, 2), 0: (3,), 1: (4,), 2: (5,), 3: (6,), 4: (7, 8), 5: (9,), 6: (10,), 7: (11,), "sum": (12,), "share": (13, 14), 8: (16,), 9: (17,), 10: (18,), 11: (19,), 12: (20,), 13: (21,), "top": (15,)}
-RELAY_AT = {0: (0, 1), 1: (2,), 2: (3,), 3: (4,), 4: (5,), 5: (6, 7), 6: (8,), 7: (9, 10), "share": (11, 12), "top": (13, 14), 8: (15,), 9: (16,), 10: (17,), 11: (18,), 12: (19,), 13: (20,), 14: (21,)}
-ARRIVE_AT = {0: (0,), 1: (1,), 2: (2,), 3: (3,), 4: (4,), 5: (5,), 6: (6,), 7: (7, 8), "end": (9, 10), "top": (11, 12, 13, 14), 8: (15,), 9: (16,), 10: (17,), 11: (18,), 12: (19,), 13: (20,), 14: (21,)}
+SEND_AT = {-1: (0, 1, 2), 0: (3,), 1: (4,), 2: (5,), 3: (6,), 4: (7, 8), 5: (9,), 6: (10,), 7: (11,), "sum": (12,), "share": (13, 14), "top": (15, 16), 8: (17, 18), 9: (19, 20), 10: (21,)}
+RELAY_AT = {0: (0, 1), 1: (2,), 2: (3,), 3: (4,), 4: (5,), 5: (6, 7), 6: (8,), 7: (9, 10), "sum": (11,), "share": (12,), "top": (13, 14, 15), 8: (16, 17), 9: (18, 19), 10: (20, 21)}
+ARRIVE_AT = {0: (0,), 1: (1,), 2: (2,), 3: (3,), 4: (4,), 5: (5,), 6: (6,), 7: (7, 8), "end": (9, 10), "ties": (11,), "top": (12, 13, 14, 15), 8: (16, 17), 9: (18, 19), 10: (20, 21)}
 
 
 def halves(value):
@@ -59,6 +59,8 @@
     swap,
     blockh,
     blockl,
+    ties,
+    pairs,
     tsol,
     tsolh,
     tsoll,
@@ -87,6 +89,8 @@
     rsem_p,
     ssem_q,
     rsem_q,
+    ssem_e,
+    rsem_e,
 ):
     leaf = lax.axis_index("leaf")
     row = lax.axis_index("prow")
@@ -153,14 +157,14 @@
             return lambda s: lower.at[t, :, s], lowers.at[owner, t]
         if p < 11:
             return None
-        if p < 15:
-            i = pl.ds(2 * (p - 11), 2)
+        if p == 11:
+            return lambda s: factor.at[s, 2 * owner, :, pl.ds(256, 256)], ties.at[owner, row]
+        if p < 16:
+            i = pl.ds(2 * (p - 12), 2)
             return lambda s: upper.at[s, i], uppers.at[owner, i]
         i = 21 - p
-        if i > 2 * owner:
+        if i >= 2 * owner:
             return None
-        if i == 2 * owner:
-            return lambda s: factor.at[s, i, :, pl.ds(256, 256)], slab.at[owner, i, :, pl.ds(256, 256)]
         return lambda s: factor.at[s, i], slab.at[owner, i]
 
     def travel(sends=(), relays=(), arrivals=(), first=False, last=False):
@@ -285,25 +289,69 @@
     def prepare_inverse(n):
         for d in range(4):
             arrived(inv.at[0, 0], rsem_i.at[n, d])
-        whole = inv[n].reshape(256, 256).T
-        invh[n % 2], invl[n % 2] = halves(whole)
+        invh[n], invl[n] = halves(inv[n].reshape(256, 256).T)
+
+    def send_ties():
+        ref = ties.at[:, row]
+        for d in (1, 2, 3):
+            remote(ref, ref, ssem_e.at[d - 1], rsem_e.at[d - 1], zpeer(d)).start()
 
     def sub_block(i, k):
         return slab[k // 2, i, :, (k % 2) * 256 : (k % 2) * 256 + 256]
 
     def terms(n):
-        if n < 8:
-            return [(lambda k=k: sub_block(n, k), k) for k in range(n)]
-        i = 15 - n
-        return [(lambda k=k: sub_block(i, k), 15 - k) for k in range(7, i, -1)]
+        return [(lambda k=k: sub_block(n, k), k) for k in range(n)]
 
     def apply(block, n):
         return product(halves(block()), (solh[n], soll[n]))
 
     def base_of(n):
-        if n < 8:
-            return base[n]
-        return sol[15 - n, rows] - coup[15 - n]
+        return base[n]
+
+    def pair_product(p, q):
+        wide_block = slab[q, 2 * p : 2 * p + 2].reshape(128, 512)
+        found = (
+            jnp.concatenate([solh[8 + 2 * q], solh[9 + 2 * q]], axis=0),
+            jnp.concatenate([soll[8 + 2 * q], soll[9 + 2 * q]], axis=0),
+        )
+        return product(halves(wide_block), found)
+
+    def pair_base(p):
+        value = jnp.concatenate([sol[2 * p, rows], sol[2 * p + 1, rows]], axis=0)
+        return value - coup[2 * p : 2 * p + 2].reshape(128, 128)
+
+    def start_pair(p, value):
+        pairs[p, 0, rows] = value[:64]
+        pairs[p, 1, rows] = value[64:]
+        ref = pairs.at[p, :, rows]
+        for d in (1, 2, 3):
+            remote(ref, ref, ssem_g.at[8 + p, d - 1], rsem_g.at[8 + p, d - 1], zpeer(d)).start()
+
+    def solve_pair(p):
+        for d in (1, 2, 3):
+            arrived(pairs.at[0, :, pl.ds(0, 64)], rsem_g.at[8 + p, d - 1])
+        tie = halves(ties[p].reshape(256, 256))
+        upper_n, lower_n = 15 - (2 * p + 1), 15 - 2 * p
+        later = product((invh[upper_n], invl[upper_n]), halves(pairs[p, 1]))
+        later_parts = halves(later)
+        right = pairs[p, 0] - product(tie, later_parts)
+        sooner = product((invh[lower_n], invl[lower_n]), halves(right))
+        sol[9 + 2 * p] = later
+        solh[9 + 2 * p], soll[9 + 2 * p] = later_parts
+        sol[8 + 2 * p] = sooner
+        solh[8 + 2 * p], soll[8 + 2 * p] = halves(sooner)
+
+    def give_out(i):
+        o = i // 2
+        place = sub_out.at[0, sub, i % 2, :, pl.ds(pl.multiple_of(half * 128, 128), 128)]
+
+        @pl.when(col == o)
+        def _():
+            pltpu.make_async_copy(sol.at[8 + i], place, rsem_o.at[i % 2, col]).start()
+
+        @pl.when(col != o)
+        def _():
+            remote(sol.at[8 + i], place, ssem_o.at[i], rsem_o.at[i % 2, col], ypeer(o)).start()
 
     def before(n):
         value = base_of(n)
@@ -326,7 +374,7 @@
     def solve(n):
         for d in (1, 2, 3):
             arrived(gath.at[0, pl.ds(0, 64)], rsem_g.at[n, d - 1])
-        value = product((invh[n % 2], invl[n % 2]), halves(gath[n]))
+        value = product((invh[n], invl[n]), halves(gath[n]))
         sol[n] = value
         solh[n], soll[n] = halves(value)
 
@@ -365,50 +413,9 @@
     base_copy.wait()
     carried = base_of(0)
 
-    for n in range(16):
-        if n == 8:
-            contrib(3)
-            at("end")
-            contrib(0)
-            me = sub * 8 + leaf
-            red[pl.ds(me, 1)] = part[pl.ds(me, 1)]
-            for k, (o, d) in enumerate(group):
-                peer, m = member(o, d)
-                remote(part.at[m], red.at[me], ssem_r.at[k], rsem_r.at[k], peer).start()
-            at("sum")
-            hand_top(1)
-            hand_top(3)
-            for k in range(15):
-                arrived(red.at[0], rsem_r.at[k])
-            total = red[0]
-            for m in range(1, 16):
-                total = total + red[m]
-            slot = sub * 4 + mine_t
-            trhs[core, row, pl.ds(slot, 1)] = -total[None]
-            ref = trhs.at[core, row, slot]
-            for k, peer in enumerate(wide):
-                remote(ref, ref, ssem_a.at[k], rsem_a.at[k], peer).start()
-            hand_top(2)
-            at("share")
-            prepare_top()
-            for k in range(31):
-                arrived(red.at[0], rsem_a.at[k])
-            remote(trhs.at[core], trhs.at[core], ssem_q.at[0], rsem_q.at[0], partner).start()
-            arrived(trhs.at[0], rsem_q.at[0])
-            solve_top()
-            for o in range(4):
-
-                @pl.when(col == o)
-                def _():
-                    remote(tsol.at[o ^ 1], swap, ssem_x.at[0], rsem_x.at[0], ypeer(o ^ 1)).start()
-
-            at("top")
-            value = sol[7, rows] - couple(7, 8)[0]
-        else:
-            value = finish(n, carried)
-        start_gather(n, value)
-        if n + 2 < 16:
-            send_inverse(n + 2)
+    for n in range(8):
+        start_gather(n, finish(n, carried))
+        send_inverse(n + 2)
         travel(sends=SEND_AT.get(n, ()), relays=RELAY_AT.get(n, ()))
         prepare_inverse(n)
         if n == 0:
@@ -418,25 +425,85 @@
         travel(arrivals=ARRIVE_AT.get(n, ()))
         if n == 7:
             contrib(2)
-        if n == 8:
-            coup[0:7] = couple(0, 7)
-        if n + 1 not in (8, 16):
+        else:
             carried = before(n + 1)
         if n == 7:
             contrib(1)
         solve(n)
-        if n >= 8:
-            i = 15 - n
-            o = i // 2
-            place = sub_out.at[0, sub, i % 2, :, pl.ds(pl.multiple_of(half * 128, 128), 128)]
-
-            @pl.when(col == o)
-            def _():
-                pltpu.make_async_copy(sol.at[n], place, rsem_o.at[i % 2, col]).start()
-
-            @pl.when(col != o)
-            def _():
-                remote(sol.at[n], place, ssem_o.at[i], rsem_o.at[i % 2, col], ypeer(o)).start()
+
+    contrib(3)
+    at("end")
+    contrib(0)
+    me = sub * 8 + leaf
+    red[pl.ds(me, 1)] = part[pl.ds(me, 1)]
+    for k, (o, d) in enumerate(group):
+        peer, m = member(o, d)
+        remote(part.at[m], red.at[me], ssem_r.at[k], rsem_r.at[k], peer).start()
+    at("sum")
+    send_inverse(10)
+    send_inverse(11)
+    hand_top(1)
+    hand_top(3)
+    for k in range(15):
+        arrived(red.at[0], rsem_r.at[k])
+    total = red[0]
+    for m in range(1, 16):
+        total = total + red[m]
+    slot = sub * 4 + mine_t
+    trhs[core, row, pl.ds(slot, 1)] = -total[None]
+    ref = trhs.at[core, row, slot]
+    for k, peer in enumerate(wide):
+        remote(ref, ref, ssem_a.at[k], rsem_a.at[k], peer).start()
+    hand_top(2)
+    at("share")
+    send_inverse(12)
+    send_inverse(13)
+    prepare_top()
+    prepare_inverse(8)
+    prepare_inverse(9)
+    at("ties")
+    send_ties()
+    for k in range(31):
+        arrived(red.at[0], rsem_a.at[k])
+    remote(trhs.at[core], trhs.at[core], ssem_q.at[0], rsem_q.at[0], partner).start()
+    arrived(trhs.at[0], rsem_q.at[0])
+    solve_top()
+    for o in range(4):
+
+        @pl.when(col == o)
+        def _():
+            remote(tsol.at[o ^ 1], swap, ssem_x.at[0], rsem_x.at[0], ypeer(o ^ 1)).start()
+
+    send_inverse(14)
+    send_inverse(15)
+    at("top")
+
+    coup[6:8] = couple(6, 8)
+    carried = pair_base(3)
+    for p in (3, 2, 1, 0):
+        n = 11 - p
+        value = carried
+        if p < 3:
+            value = value - pair_product(p, p + 1)
+        start_pair(p, value)
+        travel(sends=SEND_AT.get(n, ()), relays=RELAY_AT.get(n, ()))
+        if p == 3:
+            for d in range(3):
+                arrived(ties.at[:, 0], rsem_e.at[d])
+            coup[0:6] = couple(0, 6)
+        else:
+            give_out(2 * p + 3)
+            give_out(2 * p + 2)
+        if p:
+            prepare_inverse(15 - (2 * p - 1))
+            prepare_inverse(15 - (2 * p - 2))
+            travel(arrivals=ARRIVE_AT.get(n, ()))
+            carried = pair_base(p - 1)
+            for q in range(3, p, -1):
+                carried = carried - pair_product(p - 1, q)
+        solve_pair(p)
+    give_out(1)
+    give_out(0)
 
     arrived(swap, rsem_x.at[0])
     top = jnp.where(leaf // 4 == half, tsol[col], swap[...])
@@ -450,7 +517,14 @@
     for n in range(16):
         for d in range(3):
             arrived(inv.at[0, 0], ssem_i.at[n, d])
+    for n in range(8):
+        for d in range(3):
             arrived(gath.at[0, pl.ds(0, 64)], ssem_g.at[n, d])
+    for p in range(4):
+        for d in range(3):
+            arrived(pairs.at[0, :, pl.ds(0, 64)], ssem_g.at[8 + p, d])
+    for d in range(3):
+        arrived(ties.at[:, 0], ssem_e.at[d])
     for k in range(15):
         arrived(red.at[0], ssem_r.at[k])
     for k in range(31):
@@ -498,12 +572,12 @@
             pltpu.VMEM((4, 2, 6, 4, 32, 256), F32),
             pltpu.VMEM((16, 4, 64, 256), F32),
             pltpu.VMEM((8, 64, 128), F32),
-            pltpu.VMEM((16, 256, 128), F32),
+            pltpu.VMEM((8, 256, 128), F32),
             pltpu.VMEM((16, 256, 128), F32),
             pltpu.VMEM((16, 256, 128), BF16),
             pltpu.VMEM((16, 256, 128), BF16),
-            pltpu.VMEM((2, 256, 256), BF16),
-            pltpu.VMEM((2, 256, 256), BF16),
+            pltpu.VMEM((16, 256, 256), BF16),
+            pltpu.VMEM((16, 256, 256), BF16),
             pltpu.VMEM((8, 64, 128), F32),
             pltpu.VMEM((16, 16, 128), F32),
             pltpu.VMEM((16, 16, 128), F32),
@@ -511,6 +585,8 @@
             pltpu.VMEM((256, 128), F32),
             pltpu.VMEM((24, 256, 256), BF16),
             pltpu.VMEM((24, 256, 256), BF16),
+            pltpu.VMEM((4, 4, 64, 256), F32),
+            pltpu.VMEM((4, 2, 256, 128), F32),
             pltpu.VMEM((4, 256, 128), F32),
             pltpu.VMEM((4, 256, 128), BF16),
             pltpu.VMEM((4, 256, 128), BF16),
@@ -539,6 +615,8 @@
             dma((4,)),
             dma((1,)),
             dma((1,)),
+            dma((3,)),
+            dma((3,)),
         ],
         compiler_params=pltpu.CompilerParams(collective_id=0, has_side_effects=True, vmem_limit_bytes=56 << 20),
     )(

time: 158 us -> 151 us (0.956)
  Pallas kernels: 154 us -> 148 us
    pallas_call x1, Pallas kernels: 154 us -> 148 us  [per_device(): pl.pallas_call(kernel, name='solve', out_shape=(jax.ShapeDtypeStruct((1,...]
where the time goes in v3:
time: 151 us
  Pallas kernels  148 us (98%)
  local copies, waits for them, and re-layouts  2.91 us (2%)
    pallas_call x1, Pallas kernels, per_device(): pl.pallas_call(kernel, name='solve', out_shape=(jax.ShapeDtypeStruct((1,...  148 us

profile of v3, /device:TPU:0, one launch (start us, length us, event | category | flops | bytes accessed | tf_op | source)
XLA Modules:
  0.0 151.2 jit_solution(695132266302639463)
XLA Ops:
  0.6 147.6 %solve.1 = (f32[1,2,2,256,256]{4,3,2,1,0:T(8,128)}, f32[1,32,256]{2,1,0:T(8,128)}) custom-call(s32[2,4]{1,0:T(2,128)} %bitcast.19, f32[2,8,64,512]{3,2,1,0:T(8,128)} %bitcast.11, f32[2,8,64,256]{3,2,1,0:T(8,128)} %bitcast.12, f32[2,8,64,256]{3,2,1,0:T(8,128)} %bitcast.13, f32[4,64,2,512]{3,2,1,0:T(2,128)} %bitcast.14, f32[2,8,64,256]{3,2,1,0:T(8,128)} %bitcast.15, ...), custom_call_target="tpu_custom_call" | custom-call | tf_op jit(solution)/shard_map/solve/pallas_call | solution.py:559
  148.3 0.0 copy-start
  148.3 2.3 %copy.15 = f32[1,2,2,256,256]{4,3,2,1,0:T(8,128)} copy(f32[1,2,2,256,256]{4,3,2,1,0:T(8,128)} %get-tuple-element.8) | data formatting | bytes 2097152
  150.6 0.0 copy-done
  150.6 0.6 copy.16
Async XLA Ops:
  148.3 2.3 %copy-start = (f32[1,32,256]{2,1,0:T(8,128)S(1)}, f32[1,32,256]{2,1,0:T(8,128)}, u32[]{:S(2)}) copy-start(f32[1,32,256]{2,1,0:T(8,128)} %get-tuple-element.5) | copy-start | bytes 98308

commit v4 on v3

--- a/solution.py
+++ b/solution.py
@@ -9,8 +9,9 @@
 F32 = jnp.float32
 BF16 = jnp.bfloat16
 NPOS = 22
-SEND_AT = {-1: (0, 1, 2), 0: (3,), 1: (4,), 2: (5,), 3: (6,), 4: (7, 8), 5: (9,), 6: (10,), 7: (11,), "sum": (12,), "share": (13, 14), "top": (15, 16), 8: (17, 18), 9: (19, 20), 10: (21,)}
-RELAY_AT = {0: (0, 1), 1: (2,), 2: (3,), 3: (4,), 4: (5,), 5: (6, 7), 6: (8,), 7: (9, 10), "sum": (11,), "share": (12,), "top": (13, 14, 15), 8: (16, 17), 9: (18, 19), 10: (20, 21)}
+OVER_AT = {-1: (0, 1, 2), 0: (3,), 1: (4,), 2: (5,), 3: (6, 7), 4: (8,), 5: (9, 10), 6: (11, 12, 13), 7: (14, 15), "share": (16, 17, 18), "top": (19, 20, 21)}
+SEND_AT = {-1: (0, 1, 2), 0: (3,), 1: (4,), 2: (5,), 3: (6,), 4: (7, 8), 5: (9,), 6: (10,), 7: (11, 12), "sum": (13, 14), "share": (15,), "top": (16, 17, 18), 8: (19, 20, 21)}
+RELAY_AT = {0: (0,), 1: (1, 2), 2: (3,), 3: (4,), 4: (5,), 5: (6, 7), 6: (8,), 7: (9, 10), "sum": (11, 12), "share": (13, 14, 15), 8: (16, 17, 18), 9: (19, 20, 21)}
 ARRIVE_AT = {0: (0,), 1: (1,), 2: (2,), 3: (3,), 4: (4,), 5: (5,), 6: (6,), 7: (7, 8), "end": (9, 10), "ties": (11,), "top": (12, 13, 14, 15), 8: (16, 17), 9: (18, 19), 10: (20, 21)}
 
 
@@ -167,7 +168,7 @@
             return None
         return lambda s: factor.at[s, i], slab.at[owner, i]
 
-    def travel(sends=(), relays=(), arrivals=(), first=False, last=False):
+    def travel(sends=(), relays=(), arrivals=(), overs=(), first=False, last=False):
         for o in range(4):
             mine, there, over = o // 2, 1 - o // 2, 3 - o
 
@@ -178,16 +179,19 @@
                         if piece(o, p):
                             src, dst = piece(o, p)
                             pltpu.make_async_copy(src(mine), dst, rsem_y.at[p, o]).start()
-                for p in sends:
+                for p in overs:
                     if piece(o, p):
                         src, dst = piece(o, p)
-                        remote(src(mine), dst, ssem_y.at[p, 0], rsem_y.at[p, o], ypeer(o ^ 1)).start()
                         remote(src(there), dst, ssem_y.at[p, 1], rsem_y.at[p, o], ypeer(over)).start()
                 for p in relays:
                     if piece(over, p):
                         dst = piece(over, p)[1]
                         arrived(dst, rsem_y.at[p, over])
                         remote(dst, dst, ssem_y.at[p, 2], rsem_y.at[p, over], ypeer(o ^ 1)).start()
+                for p in sends:
+                    if piece(o, p):
+                        src, dst = piece(o, p)
+                        remote(src(mine), dst, ssem_y.at[p, 0], rsem_y.at[p, o], ypeer(o ^ 1)).start()
                 for p in arrivals:
                     for other in (o, o ^ 1, 3 - (o ^ 1)):
                         if piece(other, p):
@@ -202,7 +206,7 @@
                             arrived(piece(over, p)[1], ssem_y.at[p, 2])
 
     def at(point):
-        travel(SEND_AT.get(point, ()), RELAY_AT.get(point, ()), ARRIVE_AT.get(point, ()))
+        travel(SEND_AT.get(point, ()), RELAY_AT.get(point, ()), ARRIVE_AT.get(point, ()), OVER_AT.get(point, ()))
 
     my_rows = pl.ds(pl.multiple_of(core * 32, 32), 32)
 
@@ -291,10 +295,10 @@
             arrived(inv.at[0, 0], rsem_i.at[n, d])
         invh[n], invl[n] = halves(inv[n].reshape(256, 256).T)
 
-    def send_ties():
-        ref = ties.at[:, row]
-        for d in (1, 2, 3):
-            remote(ref, ref, ssem_e.at[d - 1], rsem_e.at[d - 1], zpeer(d)).start()
+    def send_tie(p):
+        ref = ties.at[p, row]
+        for d in (1, 2, 3):
+            remote(ref, ref, ssem_e.at[p, d - 1], rsem_e.at[p, d - 1], zpeer(d)).start()
 
     def sub_block(i, k):
         return slab[k // 2, i, :, (k % 2) * 256 : (k % 2) * 256 + 256]
@@ -330,6 +334,8 @@
     def solve_pair(p):
         for d in (1, 2, 3):
             arrived(pairs.at[0, :, pl.ds(0, 64)], rsem_g.at[8 + p, d - 1])
+        for d in range(3):
+            arrived(ties.at[0, 0], rsem_e.at[p, d])
         tie = halves(ties[p].reshape(256, 256))
         upper_n, lower_n = 15 - (2 * p + 1), 15 - 2 * p
         later = product((invh[upper_n], invl[upper_n]), halves(pairs[p, 1]))
@@ -401,8 +407,11 @@
         rhs.at[sub, :, :, pl.ds(pl.multiple_of(half * 128, 128), 128)], base, misc.at[0]
     )
     base_copy.start()
+    travel(overs=OVER_AT[-1][:1], sends=SEND_AT[-1][:1])
+    base_copy.wait()
+    start_gather(0, base_of(0))
     send_inverse(0)
-    travel(first=True, sends=SEND_AT[-1])
+    travel(overs=OVER_AT[-1][1:], sends=SEND_AT[-1][1:], first=True)
     collect_top()
     send_inverse(1)
     quarter = lax.broadcasted_iota(jnp.int32, (256, 128), 1) // 32
@@ -410,17 +419,17 @@
     spread = jnp.concatenate([narrow] * 4, axis=1)
     here = jnp.where(jnp.logical_and(leaf // 4 == half, sub == 0), lax.rem(leaf, 4), -1)
     part[...] = -jnp.where(quarter == here, spread, 0.0).reshape(16, 16, 128)
-    base_copy.wait()
-    carried = base_of(0)
+    carried = None
 
     for n in range(8):
-        start_gather(n, finish(n, carried))
+        if n:
+            start_gather(n, finish(n, carried))
         send_inverse(n + 2)
-        travel(sends=SEND_AT.get(n, ()), relays=RELAY_AT.get(n, ()))
+        travel(sends=SEND_AT.get(n, ()), relays=RELAY_AT.get(n, ()), overs=OVER_AT.get(n, ()))
         prepare_inverse(n)
-        if n == 0:
+        if n == 2:
             collect_rows()
-        if n == 1:
+        if n == 3:
             share_top()
         travel(arrivals=ARRIVE_AT.get(n, ()))
         if n == 7:
@@ -441,7 +450,6 @@
         remote(part.at[m], red.at[me], ssem_r.at[k], rsem_r.at[k], peer).start()
     at("sum")
     send_inverse(10)
-    send_inverse(11)
     hand_top(1)
     hand_top(3)
     for k in range(15):
@@ -456,17 +464,18 @@
         remote(ref, ref, ssem_a.at[k], rsem_a.at[k], peer).start()
     hand_top(2)
     at("share")
+    send_inverse(11)
+    at("ties")
+    send_tie(3)
     send_inverse(12)
-    send_inverse(13)
     prepare_top()
     prepare_inverse(8)
     prepare_inverse(9)
-    at("ties")
-    send_ties()
     for k in range(31):
         arrived(red.at[0], rsem_a.at[k])
     remote(trhs.at[core], trhs.at[core], ssem_q.at[0], rsem_q.at[0], partner).start()
     arrived(trhs.at[0], rsem_q.at[0])
+    send_inverse(13)
     solve_top()
     for o in range(4):
 
@@ -474,8 +483,6 @@
         def _():
             remote(tsol.at[o ^ 1], swap, ssem_x.at[0], rsem_x.at[0], ypeer(o ^ 1)).start()
 
-    send_inverse(14)
-    send_inverse(15)
     at("top")
 
     coup[6:8] = couple(6, 8)
@@ -486,10 +493,12 @@
         if p < 3:
             value = value - pair_product(p, p + 1)
         start_pair(p, value)
-        travel(sends=SEND_AT.get(n, ()), relays=RELAY_AT.get(n, ()))
+        if p:
+            send_tie(p - 1)
+        if p > 1:
+            send_inverse(17 - p)
+        travel(sends=SEND_AT.get(n, ()), relays=RELAY_AT.get(n, ()), overs=OVER_AT.get(n, ()))
         if p == 3:
-            for d in range(3):
-                arrived(ties.at[:, 0], rsem_e.at[d])
             coup[0:6] = couple(0, 6)
         else:
             give_out(2 * p + 3)
@@ -523,8 +532,9 @@
     for p in range(4):
         for d in range(3):
             arrived(pairs.at[0, :, pl.ds(0, 64)], ssem_g.at[8 + p, d])
-    for d in range(3):
-        arrived(ties.at[:, 0], ssem_e.at[d])
+    for p in range(4):
+        for d in range(3):
+            arrived(ties.at[0, 0], ssem_e.at[p, d])
     for k in range(15):
         arrived(red.at[0], ssem_r.at[k])
     for k in range(31):
@@ -615,8 +625,8 @@
             dma((4,)),
             dma((1,)),
             dma((1,)),
-            dma((3,)),
-            dma((3,)),
+            dma((4, 3)),
+            dma((4, 3)),
         ],
         compiler_params=pltpu.CompilerParams(collective_id=0, has_side_effects=True, vmem_limit_bytes=56 << 20),
     )(

time: 151 us -> 142 us (0.940)
  Pallas kernels: 148 us -> 138 us
    pallas_call x1, Pallas kernels: 148 us -> 138 us  [per_device(): pl.pallas_call(kernel, name='solve', out_shape=(jax.ShapeDtypeStruct((1,...]
where the time goes in v4:
time: 142 us
  Pallas kernels  138 us (97%)
  local copies, waits for them, and re-layouts  2.91 us (2%)
    pallas_call x1, Pallas kernels, per_device(): pl.pallas_call(kernel, name='solve', out_shape=(jax.ShapeDtypeStruct((1,...  138 us
    unnamed x4, local copies, waits for them, and re-layouts  2.91 us

profile of v4, /device:TPU:0, one launch (start us, length us, event | category | flops | bytes accessed | tf_op | source)
XLA Modules:
  0.0 141.5 jit_solution(1636126865278227914)
XLA Ops:
  0.6 138.0 %solve.1 = (f32[1,2,2,256,256]{4,3,2,1,0:T(8,128)}, f32[1,32,256]{2,1,0:T(8,128)}) custom-call(s32[2,4]{1,0:T(2,128)} %bitcast.19, f32[2,8,64,512]{3,2,1,0:T(8,128)} %bitcast.11, f32[2,8,64,256]{3,2,1,0:T(8,128)} %bitcast.12, f32[2,8,64,256]{3,2,1,0:T(8,128)} %bitcast.13, f32[4,64,2,512]{3,2,1,0:T(2,128)} %bitcast.14, f32[2,8,64,256]{3,2,1,0:T(8,128)} %bitcast.15, ...), custom_call_target="tpu_custom_call" | custom-call | tf_op jit(solution)/shard_map/solve/pallas_call | solution.py:569
  138.6 0.0 copy-start
  138.6 2.3 %copy.15 = f32[1,2,2,256,256]{4,3,2,1,0:T(8,128)} copy(f32[1,2,2,256,256]{4,3,2,1,0:T(8,128)} %get-tuple-element.8) | data formatting | bytes 2097152
  140.9 0.0 copy-done
  140.9 0.6 copy.16
Async XLA Ops:
  138.6 2.3 %copy-start = (f32[1,32,256]{2,1,0:T(8,128)S(1)}, f32[1,32,256]{2,1,0:T(8,128)}, u32[]{:S(2)}) copy-start(f32[1,32,256]{2,1,0:T(8,128)} %get-tuple-element.5) | copy-start | bytes 98308

commit v5 on v4

--- a/solution.py
+++ b/solution.py
@@ -92,6 +92,8 @@
     rsem_q,
     ssem_e,
     rsem_e,
+    ssem_h,
+    rsem_h,
 ):
     leaf = lax.axis_index("leaf")
     row = lax.axis_index("prow")
@@ -232,22 +234,36 @@
             arrived(tops.at[0, 0, 0, 0], rsem_v.at[1, d])
         for d in (1, 2, 3):
             arrived(tops.at[0, 0, pl.ds(0, 4), 0], rsem_v.at[2, d])
+        for j in range(1, 4):
+            ref = tops.at[mine_t, core, lax.rem(mine_t + j, 4)]
+            for d in (1, 3, 2):
+                remote(ref, ref, ssem_w.at[j, d - 1], rsem_w.at[j, d - 1], xpeer(d)).start()
+        ref = tops.at[mine_t, core, pl.ds(4, 2)]
+        for d in (1, 3, 2):
+            remote(ref, ref, ssem_w.at[0, d - 1], rsem_w.at[0, d - 1], xpeer(d)).start()
         ref = tops.at[mine_t, core]
-        for d in (1, 3, 2):
-            remote(ref, ref, ssem_w.at[d - 1], rsem_w.at[d - 1], xpeer(d)).start()
         remote(ref, ref, ssem_p.at[0], rsem_p.at[0], partner).start()
 
     def hand_top(d):
-        arrived(tops.at[0, 0], rsem_w.at[d - 1])
-        ref = tops.at[lax.rem(mine_t + 4 - d, 4), core]
-        remote(ref, ref, ssem_p.at[d], rsem_p.at[d], partner).start()
+        arrived(tops.at[0, 0, pl.ds(0, 2)], rsem_w.at[0, d - 1])
+        for j in range(1, 4):
+            arrived(tops.at[0, 0, 0], rsem_w.at[j, d - 1])
+        there = lax.rem(mine_t + 4 - d, 4)
+        for j in range(1, 4):
+            ref = tops.at[there, core, lax.rem(there + j, 4)]
+            remote(ref, ref, ssem_h.at[j, d - 1], rsem_h.at[j, d - 1], partner).start()
+        ref = tops.at[there, core, pl.ds(4, 2)]
+        remote(ref, ref, ssem_h.at[0, d - 1], rsem_h.at[0, d - 1], partner).start()
 
     def top_block(t, u):
         return jnp.concatenate([tops[t, h, u, r] for r in range(4) for h in range(2)], axis=0)
 
     def prepare_top():
-        for d in range(4):
-            arrived(tops.at[0, 0], rsem_p.at[d])
+        arrived(tops.at[0, 0], rsem_p.at[0])
+        for d in range(3):
+            arrived(tops.at[0, 0, pl.ds(0, 2)], rsem_h.at[0, d])
+            for j in range(1, 4):
+                arrived(tops.at[0, 0, 0], rsem_h.at[j, d])
         for t in range(4):
             for u in range(4):
                 if t != u:
@@ -427,9 +443,9 @@
         send_inverse(n + 2)
         travel(sends=SEND_AT.get(n, ()), relays=RELAY_AT.get(n, ()), overs=OVER_AT.get(n, ()))
         prepare_inverse(n)
+        if n == 1:
+            collect_rows()
         if n == 2:
-            collect_rows()
-        if n == 3:
             share_top()
         travel(arrivals=ARRIVE_AT.get(n, ()))
         if n == 7:
@@ -544,9 +560,11 @@
         arrived(tops.at[0, 0, 0, 0], ssem_v.at[0, d])
         arrived(tops.at[0, 0, 0, 0], ssem_v.at[1, d])
         arrived(tops.at[0, 0, pl.ds(0, 4), 0], ssem_v.at[2, d])
-        arrived(tops.at[0, 0], ssem_w.at[d])
-    for d in range(4):
-        arrived(tops.at[0, 0], ssem_p.at[d])
+        for sem in (ssem_w, ssem_h):
+            arrived(tops.at[0, 0, pl.ds(0, 2)], sem.at[0, d])
+            for j in range(1, 4):
+                arrived(tops.at[0, 0, 0], sem.at[j, d])
+    arrived(tops.at[0, 0], ssem_p.at[0])
     arrived(trhs.at[0], ssem_q.at[0])
     arrived(swap, ssem_x.at[0])
     for i in range(8):
@@ -619,12 +637,14 @@
             dma((4,)),
             dma((3, 3)),
             dma((3, 4)),
-            dma((3,)),
-            dma((3,)),
-            dma((4,)),
-            dma((4,)),
+            dma((4, 3)),
+            dma((4, 3)),
             dma((1,)),
             dma((1,)),
+            dma((1,)),
+            dma((1,)),
+            dma((4, 3)),
+            dma((4, 3)),
             dma((4, 3)),
             dma((4, 3)),
         ],

time: 142 us -> 135 us (0.951)
  Pallas kernels: 138 us -> 131 us
    pallas_call x1, Pallas kernels: 138 us -> 131 us  [per_device(): pl.pallas_call(kernel, name='solve', out_shape=(jax.ShapeDtypeStruct((1,...]
where the time goes in v5:
time: 135 us; the launch traced here: 134 us
  Pallas kernels  131 us (97%)
  local copies, waits for them, and re-layouts  2.91 us (2%)
    pallas_call x1, Pallas kernels, per_device(): pl.pallas_call(kernel, name='solve', out_shape=(jax.ShapeDtypeStruct((1,...  131 us
    unnamed x4, local copies, waits for them, and re-layouts  2.91 us

profile of v5, /device:TPU:0, one launch (start us, length us, event | category | flops | bytes accessed | tf_op | source)
XLA Modules:
  0.0 134.3 jit_solution(1702720476540177928)
XLA Ops:
  0.6 130.8 %solve.1 = (f32[1,2,2,256,256]{4,3,2,1,0:T(8,128)}, f32[1,32,256]{2,1,0:T(8,128)}) custom-call(s32[2,4]{1,0:T(2,128)} %bitcast.19, f32[2,8,64,512]{3,2,1,0:T(8,128)} %bitcast.11, f32[2,8,64,256]{3,2,1,0:T(8,128)} %bitcast.12, f32[2,8,64,256]{3,2,1,0:T(8,128)} %bitcast.13, f32[4,64,2,512]{3,2,1,0:T(2,128)} %bitcast.14, f32[2,8,64,256]{3,2,1,0:T(8,128)} %bitcast.15, ...), custom_call_target="tpu_custom_call" | custom-call | tf_op jit(solution)/shard_map/solve/pallas_call | solution.py:587
  131.4 0.0 copy-start
  131.4 2.3 %copy.15 = f32[1,2,2,256,256]{4,3,2,1,0:T(8,128)} copy(f32[1,2,2,256,256]{4,3,2,1,0:T(8,128)} %get-tuple-element.8) | data formatting | bytes 2097152
  133.7 0.0 copy-done
  133.7 0.6 copy.16
Async XLA Ops:
  131.4 2.3 %copy-start = (f32[1,32,256]{2,1,0:T(8,128)S(1)}, f32[1,32,256]{2,1,0:T(8,128)}, u32[]{:S(2)}) copy-start(f32[1,32,256]{2,1,0:T(8,128)} %get-tuple-element.5) | copy-start | bytes 98308
